TPU v7x, 128 devices: a whole 4x4x4 slice. The times are simulated.
128 devices in a mesh: seq: 4 (over z), exp: 32 (over y, x, core).
Axes of the slice: x: 4, y: 4, z: 4, core: 2. Of those that a mesh axis runs over, the one named last changes fastest.
Arguments:
- queries: bfloat16 [32, 256, 4096], P('exp', 'seq'), may hold values from -30 to 30
- key_heads: bfloat16 [32, 256, 512], P('exp', 'seq'), may hold values from -12 to 12
- value_heads: bfloat16 [32, 256, 512], P('exp', 'seq'), may hold values from -6 to 6
- residual: bfloat16 [32, 256, 4096], P('exp', 'seq'), may hold values from -16 to 16
- lengths: int32 [32, 6], P('exp'), may hold values from 1 to 128, 256 in all within a row
- routes: int32 [32, 256, 4], P('exp', 'seq'), may hold values from 0 to 31, all different within a row; in each aligned block of 64 rows (0 to 63, 64 to 127, ..., all dimensions but the last counted through in order) at most 10 rows name the same one
- gate_weights: bfloat16 [32, 256, 8], P('exp', 'seq'), may hold values from 0.049804688 to 0.29882812
- out_weight: bfloat16 [4096, 4096], P('seq', 'exp'), may hold values from -0.09375 to 0.09375
- norm_gain: float32 [4096], replicated, may hold values from 0.5 to 1.5
- w_gate: bfloat16 [32, 4, 4096, 768], P('exp', 'seq'), may hold values from -0.09375 to 0.09375
- w_up: bfloat16 [32, 4, 4096, 768], P('exp', 'seq'), may hold values from -0.09375 to 0.09375
- w_down: bfloat16 [32, 4, 768, 4096], P('exp', 'seq'), may hold values from -0.15625 to 0.15625
Outputs:
- result: bfloat16 [32, 256, 4096], P('exp', 'seq')
Inputs may be any that keep to these rules, and one draw needn't show every extreme that they name: `lengths`: each row sums to 256, and its largest entry is 128. `routes`: the 4 entries of a token differ; among the rows of one device no column is named more than 10 times, a bound that some block reaches.
All inputs are finite; a program needn't handle non-finite values.
Results may differ from a plain program's by a relative error of at most 0.008.
Values may be sent and summed in bfloat16 or wider, within the bound.
No kernel may reach another device: no remote copies, remote signals or barrier semaphores. Data moves between devices by JAX's collectives and lax.ppermute only.
A program may use at most 128 MiB of HBM per device.

v0:
```python
import functools
import math

import jax
import jax.numpy as jnp
from jax import lax
from jax.experimental import pallas as pl
from jax.experimental.pallas import tpu as pltpu
from jax.sharding import PartitionSpec as P

HEAD_DIM = 128
EXP_COL = 2


epsilon = 1e-06


def episode_ids(length_row, position_count):
    bounds = jnp.cumsum(length_row)
    position = jnp.arange(position_count, dtype=jnp.int32)
    return jnp.sum((position[:, None] >= bounds[None, :]).astype(jnp.int32), axis=1)


def attend(query_rows, key_rows, value_rows, episode):
    row_count = query_rows.shape[0]
    groups = key_rows.shape[1] // HEAD_DIM
    per_group = query_rows.shape[1] // HEAD_DIM // groups
    q_heads = query_rows.reshape(row_count, groups, per_group, HEAD_DIM)
    k_heads = key_rows.reshape(row_count, groups, HEAD_DIM)
    v_heads = value_rows.reshape(row_count, groups, HEAD_DIM)
    scores = jnp.einsum(
        "tgpd,ugd->gptu", q_heads, k_heads, preferred_element_type=jnp.float32
    ) / math.sqrt(HEAD_DIM)
    position = jnp.arange(row_count, dtype=jnp.int32)
    allowed = (episode[:, None] == episode[None, :]) & (position[None, :] <= position[:, None])
    scores = jnp.where(allowed, scores, -jnp.inf)
    row_maximum = jnp.max(scores, axis=-1, keepdims=True)
    weights = jnp.exp(scores - row_maximum)
    probability = (weights / jnp.sum(weights, axis=-1, keepdims=True)).astype(jnp.bfloat16)
    mixed = jnp.einsum("gptu,ugd->tgpd", probability, v_heads, preferred_element_type=jnp.float32)
    return mixed.astype(jnp.bfloat16).reshape(row_count, groups * per_group * HEAD_DIM)


SHARED_SLOTS = 6
TILE_ROWS = 8


HIDDEN_BLOCK = 256
OUT_BLOCK = 1024


def expert_kernel(hidden_steps, rows_ref, gate_ref, wg_ref, wu_ref, wd_ref, out_ref, act_ref):
    step = pl.program_id(0)

    @pl.when(step < hidden_steps)
    def _():
        x = rows_ref[...]
        g = jnp.dot(x, wg_ref[...], preferred_element_type=jnp.float32)
        u = jnp.dot(x, wu_ref[...], preferred_element_type=jnp.float32)
        act_ref[step] = (g / (1.0 + jnp.exp(-g)) * u).astype(jnp.bfloat16)

    @pl.when(step >= hidden_steps)
    def _():
        y = sum(
            jnp.dot(
                act_ref[b],
                wd_ref[pl.ds(b * HIDDEN_BLOCK, HIDDEN_BLOCK)],
                preferred_element_type=jnp.float32,
            )
            for b in range(hidden_steps)
        )
        y = y.astype(jnp.bfloat16).astype(jnp.float32) * gate_ref[...]
        out_ref[...] = y.astype(jnp.bfloat16)


def expert(rows, gate, w_gate, w_up, w_down):
    width, ff = w_gate.shape
    total = rows.shape[0]
    hidden_steps, out_steps = ff // HIDDEN_BLOCK, width // OUT_BLOCK

    def hidden_map(i):
        return (0, jnp.minimum(i, hidden_steps - 1))

    def out_map(i):
        return (0, jnp.maximum(i - hidden_steps, 0))

    return pl.pallas_call(
        functools.partial(expert_kernel, hidden_steps),
        grid=(hidden_steps + out_steps,),
        in_specs=[
            pl.BlockSpec((total, width), lambda i: (0, 0), pipeline_mode=pl.Buffered(1)),
            pl.BlockSpec((total, 1), lambda i: (0, 0), pipeline_mode=pl.Buffered(1)),
            pl.BlockSpec((width, HIDDEN_BLOCK), hidden_map),
            pl.BlockSpec((width, HIDDEN_BLOCK), hidden_map),
            pl.BlockSpec((ff, OUT_BLOCK), out_map),
        ],
        out_specs=pl.BlockSpec((total, OUT_BLOCK), out_map),
        out_shape=jax.ShapeDtypeStruct((total, width), jnp.bfloat16),
        scratch_shapes=[pltpu.VMEM((hidden_steps, total, HIDDEN_BLOCK), jnp.bfloat16)],
        compiler_params=pltpu.CompilerParams(vmem_limit_bytes=50 * 1024 * 1024),
        cost_estimate=pl.CostEstimate(
            flops=6 * total * width * ff,
            transcendentals=total * ff,
            bytes_accessed=2 * (3 * width * ff + 2 * total * width),
        ),
        name="expert",
    )(rows, gate, w_gate, w_up, w_down)


def ring(rows, step):
    count = lax.axis_size("seq")
    return lax.ppermute(rows, "seq", [(i, (i + step) % count) for i in range(count)])


def around(rows):
    return [rows] + [ring(rows, -k) for k in range(1, lax.axis_size("seq"))]


def in_order(parts):
    count = len(parts)
    start = lax.rem(count - lax.axis_index("seq"), count)
    return lax.dynamic_slice_in_dim(jnp.stack(parts + parts), start, count, axis=0)


def across(blocks):
    return lax.all_to_all(blocks, "exp", split_axis=0, concat_axis=0, tiled=True)


def across_slots(blocks):
    columns, slots, width = blocks.shape
    flat = blocks.reshape(columns, slots * TILE_ROWS, width // TILE_ROWS)
    return across(flat).reshape(columns, slots, width)


def local(
    queries,
    key_heads,
    value_heads,
    residual,
    lengths,
    routes,
    gate_weights,
    out_weight,
    norm_gain,
    w_gate,
    w_up,
    w_down,
):
    columns = lax.axis_size("exp")
    token_count = residual.shape[1]
    model_width = residual.shape[2]

    routed = routes[0]
    node_count = routed.shape[1]
    capacity = max(2, 5 * token_count * node_count // (4 * columns))
    column = jnp.arange(columns, dtype=jnp.int32)
    slot = jnp.arange(capacity, dtype=jnp.int32)

    def slots_of(named):
        on_node = named[:, :, None] == column[None, None, :]
        member = jnp.sum(on_node.astype(jnp.int32), axis=1)
        before = jnp.cumsum(member, axis=0) - member
        return on_node, (before[:, :, None] == slot[None, None, :]) & (member[:, :, None] > 0)

    on_node, lookup = slots_of(routed)
    lookups = [slots_of(named)[1] for named in around(routed)]
    gate_pair = gate_weights[0].reshape(token_count, node_count, EXP_COL).astype(jnp.float32)
    node_route_gate = jnp.einsum(
        "tnc,tne->tce", on_node.astype(jnp.float32), gate_pair, precision=lax.Precision.HIGHEST
    )
    slot_gate = jnp.einsum(
        "qnr,qny->nyr",
        lookup.astype(jnp.float32),
        node_route_gate,
        precision=lax.Precision.HIGHEST,
    ).astype(jnp.bfloat16)
    gate_in = across(slot_gate.reshape(columns, EXP_COL * capacity))
    expert_pick = lax.axis_index("seq") // (lax.axis_size("seq") // EXP_COL)
    gates = [
        lax.dynamic_index_in_dim(
            g.reshape(columns, EXP_COL, capacity), expert_pick, axis=1, keepdims=False
        ).astype(jnp.float32)
        for g in around(gate_in)
    ]
    direct = capacity - SHARED_SLOTS
    shared_mask = lookup[:, :, :SHARED_SLOTS].astype(jnp.bfloat16)
    shared_gate = in_order([g[:, :SHARED_SLOTS].reshape(-1) for g in gates]).reshape(-1, 1)
    direct_gate = jnp.stack([g[:, SHARED_SLOTS:] for g in gates], axis=1).reshape(-1, 1)
    offset = jnp.arange(len(lookups))
    direct_masks = [
        (m[:, :, None, SHARED_SLOTS:] & (offset[None, None, :, None] == i))
        .reshape(token_count, -1)
        .astype(jnp.bfloat16)
        for i, m in enumerate(lookups)
    ]
    send_mask = jnp.concatenate(direct_masks, axis=0)
    sum_mask = in_order(direct_masks).reshape(send_mask.shape)

    whole_q, whole_k, whole_v = (
        lax.all_to_all(queries[0], "seq", split_axis=1, concat_axis=0, tiled=True),
        lax.all_to_all(key_heads[0], "seq", split_axis=1, concat_axis=0, tiled=True),
        lax.all_to_all(value_heads[0], "seq", split_axis=1, concat_axis=0, tiled=True),
    )
    episode = episode_ids(lengths[0], whole_q.shape[0])
    mixed = attend(whole_q, whole_k, whole_v, episode)
    mixed, shared_gate, direct_gate, send_mask, sum_mask = lax.optimization_barrier(
        (mixed, shared_gate, direct_gate, send_mask, sum_mask)
    )
    head_partial = jnp.dot(
        mixed,
        lax.all_gather(out_weight, "exp", axis=1, tiled=True),
        preferred_element_type=jnp.float32,
    )
    projected = lax.psum_scatter(
        head_partial.astype(jnp.bfloat16), "seq", scatter_dimension=0, tiled=True
    ).astype(jnp.float32)
    hidden = residual[0].astype(jnp.float32) + projected
    inverse = lax.rsqrt(jnp.mean(hidden * hidden, axis=1, keepdims=True) + epsilon)
    normalized_rows = (hidden * inverse * norm_gain[None, :]).astype(jnp.bfloat16)

    gate_block, up_block, down_block = w_gate[0, 0], w_up[0, 0], w_down[0, 0]
    weights = (gate_block, up_block, down_block)
    shared_out = jnp.einsum(
        "roj,rm->ojm", shared_mask, normalized_rows, preferred_element_type=jnp.float32
    ).astype(jnp.bfloat16)
    shared_in, pack_rows = lax.optimization_barrier(
        (across_slots(shared_out).reshape(-1, model_width), around(normalized_rows))
    )
    shared_rows = lax.all_gather(shared_in, "seq", axis=0, tiled=True)
    direct_out = jnp.einsum(
        "rq,rm->qm",
        send_mask,
        jnp.concatenate(pack_rows, axis=0),
        preferred_element_type=jnp.float32,
    ).astype(jnp.bfloat16)
    direct_count = direct_out.shape[0]
    direct_rows = across(direct_out.reshape(columns, -1, model_width))
    shared_rows, direct_rows = lax.optimization_barrier((shared_rows, direct_rows))
    shared_parts = expert(shared_rows, shared_gate, *weights)
    direct_parts = expert(direct_rows.reshape(direct_count, model_width), direct_gate, *weights)
    direct_back = across(direct_parts.reshape(columns, -1, model_width))
    shared_sums = lax.psum_scatter(shared_parts, "seq", scatter_dimension=0, tiled=True)
    shared_sums, direct_back = lax.optimization_barrier((shared_sums, direct_back))
    shared_back = across_slots(shared_sums.reshape(columns, SHARED_SLOTS, model_width))
    pack_sums = jnp.einsum(
        "rq,qm->rm",
        sum_mask,
        direct_back.reshape(direct_count, model_width),
        preferred_element_type=jnp.float32,
    ).astype(jnp.bfloat16)
    direct_sums = lax.psum_scatter(pack_sums, "seq", scatter_dimension=0, tiled=True)
    total = hidden + jnp.einsum(
        "gyr,yre->ge", shared_mask, shared_back, preferred_element_type=jnp.float32
    )
    total = total + direct_sums.astype(jnp.float32)
    return total.astype(jnp.bfloat16)[None]


def solution(mesh):
    return jax.shard_map(
        local,
        mesh=mesh,
        in_specs=(
            P("exp", "seq", None),
            P("exp", "seq", None),
            P("exp", "seq", None),
            P("exp", "seq", None),
            P("exp", None),
            P("exp", "seq", None),
            P("exp", "seq", None),
            P("seq", "exp"),
            P(),
            P("exp", "seq", None, None),
            P("exp", "seq", None, None),
            P("exp", "seq", None, None),
        ),
        out_specs=P("exp", "seq", None),
        check_vma=False,
    )
```

profile of v0, /device:TPU:1, one launch (start us, length us, event | category | flops | bytes accessed | tf_op | source)
XLA Modules:
  0.0 365.2 jit_solution(6676005759407289215)
XLA Ops:
  7.3 4.7 %collective-permute-start.3 = (s32[64,4]{0,1:T(4,128)}, s32[64,4]{0,1:T(4,128)S(1)}, u32[]{:S(2)}, u32[]{:S(2)}) collective-permute-start(s32[64,4]{0,1:T(4,128)} %bitcast.131), channel_id=1, source_target_pairs={{0,96},{32,0},{64,32},{96,64},{1,97},{33,1},{65,33},{97,65},{2,98}... | collective-permute-start | bytes 3080 | tf_op jit(solution)/shard_map/ppermute | solution.py:112
  16.1 8.6 %all-to-all-start.3 = ((bf16[32,1,20]{2,1,0:T(2,128)(2,1)}), bf16[32,1,20]{2,1,0:T(2,128)(2,1)S(1)}, u32[]{:S(2)}, u32[]{:S(2)}) async-start(bf16[32,1,20]{2,1,0:T(2,128)(2,1)} %reshape.410), calls=%async_computation.3 | async-start | bytes 32768 | tf_op jit(solution)/shard_map/all_to_all | solution.py:126
  33.6 3.5 all-to-all-start.1
  37.2 1.9 collective-permute-start.2
  39.1 1.9 collective-permute-start.1
  43.3 3.2 collective-permute-done.1
  47.3 3.3 all-to-all-start
  51.1 4.0 %all-to-all-done = bf16[64,4,128]{2,0,1:T(8,128)(2,1)S(1)} async-done(((bf16[64,4,128]{2,0,1:T(8,128)(2,1)}), bf16[64,4,128]{2,0,1:T(8,128)(2,1)S(1)}, u32[]{:S(2)}, u32[]{:S(2)}) %all-to-all-start) | async-done | bytes 65568 | tf_op jit(solution)/shard_map/all_to_all | solution.py:201
  55.1 3.3 all-to-all-start.2
  59.4 3.5 all-to-all-done.2
  63.4 9.3 %all-gather.3.cloned.1.call-done = bf16[1024,4096]{1,0:T(8,128)(2,1)} async-done(((bf16[1024,128]{1,0:T(8,128)(2,1)}), bf16[1024,4096]{1,0:T(8,128)(2,1)}) %all-gather.3.cloned.1.call-update) | async-done | bytes 8388624 | tf_op jit(solution)/shard_map/all_gather | solution.py:211
  72.7 7.1 %convolution_convert_fusion.1 = bf16[256,4096]{1,0:T(8,128)(2,1)} fusion(bf16[256,1024]{0,1:T(8,128)(2,1)S(1)} %bitcast.123, bf16[1024,4096]{1,0:T(8,128)(2,1)} %all-gather.3.cloned.1.call-done), kind=kOutput, calls=%fused_computation.1 | convolution fusion | flops 2148532224 | bytes 11010048 | tf_op jit(solution)/shard_map/dot_general | solution.py:209
  79.8 29.4 %reduce-scatter.4.cloned.1.call-done = bf16[64,4096]{1,0:T(8,128)(2,1)} async-done(((bf16[256,4096]{1,0:T(8,128)(2,1)}), bf16[64,4096]{1,0:T(8,128)(2,1)}) %reduce-scatter.4.cloned.1.call-update) | async-done | bytes 524304 | tf_op jit(solution)/shard_map/reduce_scatter | solution.py:214
  109.3 1.3 multiply_reduce_fusion
  110.6 1.2 multiply_convert_fusion
  113.3 2.8 reshape.394
  116.1 7.5 %all-to-all-start.4 = ((bf16[32,48,512]{2,1,0:T(8,128)(2,1)}), bf16[32,48,512]{2,1,0:T(8,128)(2,1)S(1)}, u32[]{:S(2)}, u32[]{:S(2)}) async-start(bf16[32,48,512]{2,1,0:T(8,128)(2,1)} %reshape.394), calls=%async_computation.5 | async-start | bytes 3145728 | tf_op jit(solution)/shard_map/all_to_all | solution.py:126
  125.7 20.0 %all-to-all-done.4 = bf16[32,48,512]{2,1,0:T(8,128)(2,1)S(1)} async-done(((bf16[32,48,512]{2,1,0:T(8,128)(2,1)}), bf16[32,48,512]{2,1,0:T(8,128)(2,1)S(1)}, u32[]{:S(2)}, u32[]{:S(2)}) %all-to-all-start.4) | async-done | bytes 1572896 | tf_op jit(solution)/shard_map/all_to_all | solution.py:126
  145.8 2.1 reshape_reshape.6
  147.9 3.0 collective-permute-done.8
  150.9 4.6 %convolution_convert_fusion = bf16[512,4096]{1,0:T(8,128)(2,1)} fusion(bf16[256,512]{0,1:T(8,128)(2,1)S(1)} %copy-done.3, bf16[64,4096]{1,0:T(8,128)(2,1)} %collective-permute-done.8, bf16[64,4096]{1,0:T(8,128)(2,1)} %collective-permute-done.7, bf16[64,4096]{1,0:T(8,128)(2,1)} %collective-permute-done.6, bf16[64,4096]{1,0:T(8,128)(2,1)S(1)} %multiply_convert_fusion), kind=kOutput, calls=%fused_computation | convolution fusion | flops 1084227584 | bytes 6553600 | tf_op jit(solution)/shard_map/rq,rm->qm/dot_general | solution.py:230
  155.5 7.6 %all-to-all-start.5 = ((bf16[32,16,4096]{2,1,0:T(8,128)(2,1)}), bf16[32,16,4096]{2,1,0:T(8,128)(2,1)}, u32[]{:S(2)}, u32[]{:S(2)}) async-start(bf16[32,16,4096]{2,1,0:T(8,128)(2,1)} %bitcast.106), calls=%async_computation.6 | async-start | bytes 8388608 | tf_op jit(solution)/shard_map/all_to_all | solution.py:126
  163.5 49.8 %all-to-all-done.5 = bf16[32,16,4096]{2,1,0:T(8,128)(2,1)} async-done(((bf16[32,16,4096]{2,1,0:T(8,128)(2,1)}), bf16[32,16,4096]{2,1,0:T(8,128)(2,1)}, u32[]{:S(2)}, u32[]{:S(2)}) %all-to-all-start.5) | async-done | bytes 4194336 | tf_op jit(solution)/shard_map/all_to_all | solution.py:126
  213.4 3.1 all-gather.5.cloned.1.call-done.rows_ref
  216.5 23.8 %expert.2 = bf16[768,4096]{1,0:T(8,128)(2,1)} custom-call(bf16[768,4096]{1,0:T(8,128)(2,1)} %all-gather.5.cloned.1.call-done.rows_ref, f32[768,1]{1,0:T(8,128)S(1)} %copy.276.gate_ref, bf16[4096,768]{1,0:T(8,128)(2,1)} %bitcast.135, bf16[4096,768]{1,0:T(8,128)(2,1)} %bitcast.137, bf16[768,4096]{1,0:T(8,128)(2,1)} %bitcast.139), custom_call_target="tpu_custom_call" | custom-call | flops 14495514624 | bytes 31457280 | tf_op jit(solution)/shard_map/expert/pallas_call | solution.py:87
  240.5 19.0 %expert.3 = bf16[512,4096]{1,0:T(8,128)(2,1)} custom-call(bf16[512,4096]{1,0:T(8,128)(2,1)} %bitcast.46.rows_ref, f32[512,1]{1,0:T(8,128)S(1)} %copy.277.gate_ref, bf16[4096,768]{1,0:T(8,128)(2,1)} %bitcast.136, bf16[4096,768]{1,0:T(8,128)(2,1)} %bitcast.138, bf16[768,4096]{1,0:T(8,128)(2,1)} %bitcast.140), custom_call_target="tpu_custom_call" | custom-call | flops 9663676416 | bytes 27262976 | tf_op jit(solution)/shard_map/expert/pallas_call | solution.py:87
  259.5 58.7 %all_to_all.80 = bf16[32,16,4096]{2,1,0:T(8,128)(2,1)} all-to-all(bf16[32,16,4096]{2,1,0:T(8,128)(2,1)} %bitcast.108), channel_id=1, replica_groups=mesh['seq'=4,'exp'=32] {'exp'}, dimensions={0} | all-to-all | bytes 8388608 | tf_op jit(solution)/shard_map/all_to_all | solution.py:126
  318.2 4.8 %convolution_convert_fusion.2 = bf16[256,4096]{1,0:T(8,128)(2,1)} fusion(bf16[256,512]{1,0:T(8,128)(2,1)S(1)} %bitcast.124, bf16[512,4096]{1,0:T(8,128)(2,1)} %bitcast.107), kind=kOutput, calls=%fused_computation.2 | convolution fusion | flops 1074790400 | bytes 6553600 | tf_op jit(solution)/shard_map/rq,qm->rm/dot_general | solution.py:245
  323.0 2.6 reshape_reshape.7
  325.6 26.6 %all_to_all.81 = bf16[32,48,512]{2,1,0:T(8,128)(2,1)} all-to-all(bf16[32,48,512]{2,1,0:T(8,128)(2,1)S(1)} %reshape_reshape.7), channel_id=1, replica_groups=mesh['seq'=4,'exp'=32] {'exp'}, dimensions={0} | all-to-all | bytes 3145728 | tf_op jit(solution)/shard_map/all_to_all | solution.py:126
  352.3 3.5 reshape.398
  355.8 2.9 fusion.3
  (153 shorter events, 22.8 us)
Async XLA Ops:
  6.5 20.3 %copy-start.2 = (bf16[1,64,4096]{2,1,0:T(8,128)(2,1)S(1)}, bf16[1,64,4096]{2,1,0:T(8,128)(2,1)}, u32[]{:S(2)}) copy-start(bf16[1,64,4096]{2,1,0:T(8,128)(2,1)} %param.12) | copy-start | bytes 1572868
  6.5 21.7 %copy-start.4 = (bf16[1,64,512]{2,1,0:T(8,128)(2,1)S(1)}, bf16[1,64,512]{2,1,0:T(8,128)(2,1)}, u32[]{:S(2)}) copy-start(bf16[1,64,512]{2,1,0:T(8,128)(2,1)} %param.13) | copy-start | bytes 196612
  6.5 66.2 %all-gather.3.cloned.1.call-start = ((), (), s32[]{:S(2)}) async-start(), calls=%async_computation.11 | async-start | bytes 8650752 | tf_op jit(solution)/shard_map/all_gather | solution.py:211
  7.3 22.2 %collective-permute-start.3 = (s32[64,4]{0,1:T(4,128)}, s32[64,4]{0,1:T(4,128)S(1)}, u32[]{:S(2)}, u32[]{:S(2)}) collective-permute-start(s32[64,4]{0,1:T(4,128)} %bitcast.131), channel_id=1, source_target_pairs={{0,96},{32,0},{64,32},{96,64},{1,97},{33,1},{65,33},{97,65},{2,98}... | collective-permute-start | bytes 3080 | tf_op jit(solution)/shard_map/ppermute | solution.py:112
  11.9 17.6 %collective-permute-start.4 = (s32[64,4]{0,1:T(4,128)}, s32[64,4]{0,1:T(4,128)S(1)}, u32[]{:S(2)}, u32[]{:S(2)}) collective-permute-start(s32[64,4]{0,1:T(4,128)} %bitcast.132), channel_id=1, source_target_pairs={{0,64},{32,96},{64,0},{96,32},{1,65},{33,97},{65,1},{97,33},{2,66}... | collective-permute-start | bytes 3080 | tf_op jit(solution)/shard_map/ppermute | solution.py:112
  11.9 18.2 %collective-permute-start.5 = (s32[64,4]{0,1:T(4,128)}, s32[64,4]{0,1:T(4,128)S(1)}, u32[]{:S(2)}, u32[]{:S(2)}) collective-permute-start(s32[64,4]{0,1:T(4,128)} %bitcast.133), channel_id=1, source_target_pairs={{0,32},{32,64},{64,96},{96,0},{1,33},{33,65},{65,97},{97,1},{2,34}... | collective-permute-start | bytes 3080 | tf_op jit(solution)/shard_map/ppermute | solution.py:112
  13.6 15.3 %copy-start.5 = (bf16[1,64,512]{2,1,0:T(8,128)(2,1)S(1)}, bf16[1,64,512]{2,1,0:T(8,128)(2,1)}, u32[]{:S(2)}) copy-start(bf16[1,64,512]{2,1,0:T(8,128)(2,1)} %param.14) | copy-start | bytes 196612
  16.1 17.5 %all-to-all-start.3 = ((bf16[32,1,20]{2,1,0:T(2,128)(2,1)}), bf16[32,1,20]{2,1,0:T(2,128)(2,1)S(1)}, u32[]{:S(2)}, u32[]{:S(2)}) async-start(bf16[32,1,20]{2,1,0:T(2,128)(2,1)} %reshape.410), calls=%async_computation.3 | async-start | bytes 32768 | tf_op jit(solution)/shard_map/all_to_all | solution.py:126
  33.6 13.7 %all-to-all-start.1 = ((bf16[64,4,1024]{2,0,1:T(8,128)(2,1)}), bf16[64,4,1024]{2,0,1:T(8,128)(2,1)S(1)}, u32[]{:S(2)}, u32[]{:S(2)}) async-start(bf16[64,4,1024]{2,0,1:T(8,128)(2,1)} %copy.244), calls=%async_computation.1 | async-start | bytes 1048576 | tf_op jit(solution)/shard_map/all_to_all | solution.py:200
  37.2 6.1 %collective-permute-start.2 = (bf16[32,20]{0,1:T(8,128)(2,1)S(1)}, bf16[32,20]{0,1:T(8,128)(2,1)S(1)}, u32[]{:S(2)}, u32[]{:S(2)}) collective-permute-start(bf16[32,20]{0,1:T(8,128)(2,1)S(1)} %bitcast.127), channel_id=1, source_target_pairs={{0,32},{32,64},{64,96},{96,0},{1,33},{33,65},{65,97},{97,1},{2,34}... | collective-permute-start | bytes 3848 | tf_op jit(solution)/shard_map/ppermute | solution.py:112
  39.1 7.4 %collective-permute-start.1 = (bf16[32,20]{0,1:T(8,128)(2,1)S(1)}, bf16[32,20]{0,1:T(8,128)(2,1)S(1)}, u32[]{:S(2)}, u32[]{:S(2)}) collective-permute-start(bf16[32,20]{0,1:T(8,128)(2,1)S(1)} %bitcast.128), channel_id=1, source_target_pairs={{0,64},{32,96},{64,0},{96,32},{1,65},{33,97},{65,1},{97,33},{2,66}... | collective-permute-start | bytes 3848 | tf_op jit(solution)/shard_map/ppermute | solution.py:112
  41.0 5.6 %collective-permute-start = (bf16[32,20]{0,1:T(8,128)(2,1)S(1)}, bf16[32,20]{0,1:T(8,128)(2,1)S(1)}, u32[]{:S(2)}, u32[]{:S(2)}) collective-permute-start(bf16[32,20]{0,1:T(8,128)(2,1)S(1)} %bitcast.129), channel_id=1, source_target_pairs={{0,96},{32,0},{64,32},{96,64},{1,97},{33,1},{65,33},{97,65},{2,98}... | collective-permute-start | bytes 3848 | tf_op jit(solution)/shard_map/ppermute | solution.py:112
  47.3 7.7 %all-to-all-start = ((bf16[64,4,128]{2,0,1:T(8,128)(2,1)}), bf16[64,4,128]{2,0,1:T(8,128)(2,1)S(1)}, u32[]{:S(2)}, u32[]{:S(2)}) async-start(bf16[64,4,128]{2,0,1:T(8,128)(2,1)} %copy.243), calls=%async_computation | async-start | bytes 131072 | tf_op jit(solution)/shard_map/all_to_all | solution.py:201
  55.1 7.8 %all-to-all-start.2 = ((bf16[64,4,128]{2,0,1:T(8,128)(2,1)}), bf16[64,4,128]{2,0,1:T(8,128)(2,1)S(1)}, u32[]{:S(2)}, u32[]{:S(2)}) async-start(bf16[64,4,128]{2,0,1:T(8,128)(2,1)} %copy.246), calls=%async_computation.2 | async-start | bytes 131072 | tf_op jit(solution)/shard_map/all_to_all | solution.py:202
  58.4 50.9 %reduce-scatter.4.cloned.1.call-start = ((), (), s32[]{:S(2)}) async-start(), calls=%async_computation.12 | async-start | bytes 2621440 | tf_op jit(solution)/shard_map/reduce_scatter | solution.py:214
  79.8 29.5 %copy-start = (bf16[1,64,4096]{2,1,0:T(8,128)(2,1)S(1)}, bf16[1,64,4096]{2,1,0:T(8,128)(2,1)}, u32[]{:S(2)}) copy-start(bf16[1,64,4096]{2,1,0:T(8,128)(2,1)} %param.15) | copy-start | bytes 1572868
  79.8 30.8 %copy-start.6 = (f32[4096]{0:T(1024)S(1)}, f32[4096]{0:T(1024)}, u32[]{:S(2)}) copy-start(f32[4096]{0:T(1024)} %param.20) | copy-start | bytes 49156
  116.1 29.7 %all-to-all-start.4 = ((bf16[32,48,512]{2,1,0:T(8,128)(2,1)}), bf16[32,48,512]{2,1,0:T(8,128)(2,1)S(1)}, u32[]{:S(2)}, u32[]{:S(2)}) async-start(bf16[32,48,512]{2,1,0:T(8,128)(2,1)} %reshape.394), calls=%async_computation.5 | async-start | bytes 3145728 | tf_op jit(solution)/shard_map/all_to_all | solution.py:126
  123.6 27.3 %copy-start.3 = (bf16[256,512]{0,1:T(8,128)(2,1)S(1)}, bf16[256,512]{0,1:T(8,128)(2,1)}, u32[]{:S(2)}) copy-start(bf16[256,512]{0,1:T(8,128)(2,1)} %add_convert_fusion) | copy-start | bytes 786436
  123.6 92.9 %all-gather.5.cloned.1.call-start = ((), (), s32[]{:S(2)}) async-start(), calls=%async_computation.13 | async-start | bytes 7864320 | tf_op jit(solution)/shard_map/all_gather | solution.py:229
  123.6 24.3 %collective-permute-start.6 = (bf16[64,4096]{1,0:T(8,128)(2,1)S(1)}, bf16[64,4096]{1,0:T(8,128)(2,1)}, u32[]{:S(2)}, u32[]{:S(2)}) collective-permute-start(bf16[64,4096]{1,0:T(8,128)(2,1)S(1)} %multiply_convert_fusion), channel_id=1, source_target_pairs={{0,96},{32,0},{64,32},{96,64},{1,97},{33,1},{65,33},{97,65},{2,98}... | collective-permute-start | bytes 1572872 | tf_op jit(solution)/shard_map/ppermute | solution.py:112
  124.2 23.7 %collective-permute-start.7 = (bf16[64,4096]{1,0:T(8,128)(2,1)S(1)}, bf16[64,4096]{1,0:T(8,128)(2,1)}, u32[]{:S(2)}, u32[]{:S(2)}) collective-permute-start(bf16[64,4096]{1,0:T(8,128)(2,1)S(1)} %multiply_convert_fusion), channel_id=1, source_target_pairs={{0,64},{32,96},{64,0},{96,32},{1,65},{33,97},{65,1},{97,33},{2,66}... | collective-permute-start | bytes 1572872 | tf_op jit(solution)/shard_map/ppermute | solution.py:112
  125.4 25.5 %collective-permute-start.8 = (bf16[64,4096]{1,0:T(8,128)(2,1)S(1)}, bf16[64,4096]{1,0:T(8,128)(2,1)}, u32[]{:S(2)}, u32[]{:S(2)}) collective-permute-start(bf16[64,4096]{1,0:T(8,128)(2,1)S(1)} %multiply_convert_fusion), channel_id=1, source_target_pairs={{0,32},{32,64},{64,96},{96,0},{1,33},{33,65},{65,97},{97,1},{2,34}... | collective-permute-start | bytes 1572872 | tf_op jit(solution)/shard_map/ppermute | solution.py:112
  155.5 57.8 %all-to-all-start.5 = ((bf16[32,16,4096]{2,1,0:T(8,128)(2,1)}), bf16[32,16,4096]{2,1,0:T(8,128)(2,1)}, u32[]{:S(2)}, u32[]{:S(2)}) async-start(bf16[32,16,4096]{2,1,0:T(8,128)(2,1)} %bitcast.106), calls=%async_computation.6 | async-start | bytes 8388608 | tf_op jit(solution)/shard_map/all_to_all | solution.py:126
  163.1 155.2 %reduce-scatter.6.cloned.1.call-start = ((), (), s32[]{:S(2)}) async-start(), calls=%async_computation.14 | async-start | bytes 7864320 | tf_op jit(solution)/shard_map/reduce_scatter | solution.py:242
  240.3 115.4 %reduce-scatter.8.cloned.1.call-start = ((), (), s32[]{:S(2)}) async-start(), calls=%async_computation.15 | async-start | bytes 2621440 | tf_op jit(solution)/shard_map/reduce_scatter | solution.py:251
  352.3 3.5 copy-start.1
Sparse Core Ops, SparseCore 0:
  9.5 63.1 all-gather.2
  79.9 29.2 reduce-scatter.3
  151.0 65.4 all-gather.4
  240.5 64.7 reduce-scatter.5
  323.1 26.3 reduce-scatter.7
where the time goes:
time: 366 us; the launch traced here: 365 us
  waiting for transfers between devices  127 us (35%)
  blocking collectives  85.4 us (23%)
  starting transfers between devices  46.7 us (13%)
  Pallas kernels  42.8 us (12%)
  matrix products  21.5 us (6%)
  local copies, waits for them, and re-layouts  20.4 us (6%)
  between operations  13.8 us (4%)
  other arithmetic  7.54 us (2%)
    all_to_all x2, blocking collectives, across(): lax.all_to_all(blocks, 'exp', split_axis=0, concat_axis=0, tiled=True)  85.4 us
    all_to_all x3, waiting for transfers between devices, across(): lax.all_to_all(blocks, 'exp', split_axis=0, concat_axis=0, tiled=True)  69.8 us
    pallas_call x2, Pallas kernels, expert(): pl.pallas_call(functools.partial(expert_kernel, hidden_steps), grid=(hidd...  42.8 us
    reduce_scatter x1, waiting for transfers between devices, local(): lax.psum_scatter(head_partial.astype(jnp.bfloat16), 'seq', scatter_dimens...  29.4 us
    all_to_all x3, starting transfers between devices, across(): lax.all_to_all(blocks, 'exp', split_axis=0, concat_axis=0, tiled=True)  23.6 us
    ppermute x9, starting transfers between devices, ring(): lax.ppermute(rows, 'seq', [(i, (i + step) % count) for i in range(count)])  12.5 us
    all_gather x1, waiting for transfers between devices, local(): lax.all_gather(out_weight, 'exp', axis=1, tiled=True)  9.32 us
  transfers between devices with their start and end apart: 20, of which 10 were waited for; matrix products, arithmetic and copies ran while one was open for 8% of the time, Pallas kernels for 5%

commit v1 on v0

v1 whole, which is shorter than its diff:
```python
import functools
import math

import jax
import jax.numpy as jnp
from jax import lax
from jax.experimental import pallas as pl
from jax.experimental.pallas import tpu as pltpu
from jax.sharding import PartitionSpec as P

HEAD_DIM = 128
EXP_COL = 2


epsilon = 1e-06


def episode_ids(length_row, position_count):
    bounds = jnp.cumsum(length_row)
    position = jnp.arange(position_count, dtype=jnp.int32)
    return jnp.sum((position[:, None] >= bounds[None, :]).astype(jnp.int32), axis=1)


def attend(query_rows, key_rows, value_rows, episode):
    row_count = query_rows.shape[0]
    groups = key_rows.shape[1] // HEAD_DIM
    per_group = query_rows.shape[1] // HEAD_DIM // groups
    q_heads = query_rows.reshape(row_count, groups, per_group, HEAD_DIM)
    k_heads = key_rows.reshape(row_count, groups, HEAD_DIM)
    v_heads = value_rows.reshape(row_count, groups, HEAD_DIM)
    scores = jnp.einsum(
        "tgpd,ugd->gptu", q_heads, k_heads, preferred_element_type=jnp.float32
    ) / math.sqrt(HEAD_DIM)
    position = jnp.arange(row_count, dtype=jnp.int32)
    allowed = (episode[:, None] == episode[None, :]) & (position[None, :] <= position[:, None])
    scores = jnp.where(allowed, scores, -jnp.inf)
    row_maximum = jnp.max(scores, axis=-1, keepdims=True)
    weights = jnp.exp(scores - row_maximum)
    probability = (weights / jnp.sum(weights, axis=-1, keepdims=True)).astype(jnp.bfloat16)
    mixed = jnp.einsum("gptu,ugd->tgpd", probability, v_heads, preferred_element_type=jnp.float32)
    return mixed.astype(jnp.bfloat16).reshape(row_count, groups * per_group * HEAD_DIM)


SHARED_SLOTS = 6
TILE_ROWS = 8


CHUNK = 1024


def expert_kernel(sizes, places, aliased, *refs):
    count = len(sizes)
    pieces, (gate_ref, wg_ref, wu_ref, wd_ref) = refs[:count], refs[count : count + 4]
    out_ref, x_ref, wg_buf, wu_buf, wd_buf, g_ref, u_ref, y_ref, in_sems, out_sems = refs[
        count + 4 + aliased :
    ]
    chunks, out_chunks = x_ref.shape[0], wd_buf.shape[0]
    seats = out_ref.shape[0]
    seat = lax.axis_index("seq") if seats > 1 else 0

    def span(at):
        return pl.ds(pl.multiple_of(at * CHUNK, CHUNK), CHUNK)

    def loads(k):
        at = 0
        for i, size in enumerate(sizes):
            yield pltpu.make_async_copy(
                pieces[i].at[:, span(k)], x_ref.at[k, pl.ds(at, size)], in_sems.at[k, i]
            )
            at += size
        yield pltpu.make_async_copy(wg_ref.at[span(k)], wg_buf.at[k], in_sems.at[k, count])
        yield pltpu.make_async_copy(wu_ref.at[span(k)], wu_buf.at[k], in_sems.at[k, count + 1])

    def down_load(n):
        return pltpu.make_async_copy(
            wd_ref.at[:, span(n)], wd_buf.at[n], in_sems.at[n, count + 2]
        )

    def stores(n):
        slot = lax.rem(n, 2)
        for i, (offset, start, size) in enumerate(places):
            yield pltpu.make_async_copy(
                y_ref.at[slot, pl.ds(start, size)],
                out_ref.at[lax.rem(seat + offset, seats), :, span(n)],
                out_sems.at[slot, i],
            )

    for k in range(chunks):
        for c in loads(k):
            c.start()
    for n in range(out_chunks):
        down_load(n).start()

    g_ref[...] = jnp.zeros_like(g_ref)
    u_ref[...] = jnp.zeros_like(u_ref)

    def up(k, carry):
        for c in loads(k):
            c.wait()
        x = x_ref[k]
        g_ref[...] += jnp.dot(x, wg_buf[k], preferred_element_type=jnp.float32)
        u_ref[...] += jnp.dot(x, wu_buf[k], preferred_element_type=jnp.float32)
        return carry

    lax.fori_loop(0, chunks, up, 0)
    g = g_ref[...]
    act = (g / (1.0 + jnp.exp(-g)) * u_ref[...]).astype(jnp.bfloat16)

    def down(n, carry):
        down_load(n).wait()

        @pl.when(n >= 2)
        def _():
            for c in stores(n - 2):
                c.wait()

        y = jnp.dot(act, wd_buf[n], preferred_element_type=jnp.float32)
        y = y.astype(jnp.bfloat16).astype(jnp.float32) * gate_ref[...]
        y_ref[lax.rem(n, 2)] = y.astype(jnp.bfloat16)
        for c in stores(n):
            c.start()
        return carry

    lax.fori_loop(0, out_chunks, down, 0)
    for n in (out_chunks - 2, out_chunks - 1):
        for c in stores(n):
            c.wait()


def expert(pieces, gate, w_gate, w_up, w_down, seats, places, into=None):
    width, ff = w_gate.shape
    sizes = tuple(p.shape[0] for p in pieces)
    total = sum(sizes)
    chunks = width // CHUNK
    any_space = pl.BlockSpec(memory_space=pl.ANY)
    aliased = 0 if into is None else 1
    return pl.pallas_call(
        functools.partial(expert_kernel, sizes, places, aliased),
        in_specs=[any_space for _ in pieces]
        + [pl.BlockSpec(memory_space=pltpu.VMEM)]
        + [any_space] * (3 + aliased),
        out_specs=any_space,
        out_shape=jax.ShapeDtypeStruct((seats, places[0][2], width), jnp.bfloat16),
        scratch_shapes=[
            pltpu.VMEM((chunks, total, CHUNK), jnp.bfloat16),
            pltpu.VMEM((chunks, CHUNK, ff), jnp.bfloat16),
            pltpu.VMEM((chunks, CHUNK, ff), jnp.bfloat16),
            pltpu.VMEM((chunks, ff, CHUNK), jnp.bfloat16),
            pltpu.VMEM((total, ff), jnp.float32),
            pltpu.VMEM((total, ff), jnp.float32),
            pltpu.VMEM((2, total, CHUNK), jnp.bfloat16),
            pltpu.SemaphoreType.DMA((chunks, len(pieces) + 3)),
            pltpu.SemaphoreType.DMA((2, len(places))),
        ],
        input_output_aliases={len(pieces) + 4: 0} if aliased else {},
        compiler_params=pltpu.CompilerParams(vmem_limit_bytes=50 * 1024 * 1024),
        cost_estimate=pl.CostEstimate(
            flops=6 * total * width * ff,
            transcendentals=total * ff,
            bytes_accessed=2 * (3 * width * ff + 2 * total * width),
        ),
        name="expert",
    )(*pieces, gate, w_gate, w_up, w_down, *(() if into is None else (into,)))


def ring(rows, step):
    count = lax.axis_size("seq")
    return lax.ppermute(rows, "seq", [(i, (i + step) % count) for i in range(count)])


def around(rows):
    return [rows] + [ring(rows, -k) for k in range(1, lax.axis_size("seq"))]


def back_around(parts):
    return [parts[0]] + [ring(p, k) for k, p in enumerate(parts) if k]


def gather_ring(rows):
    half = rows.shape[0] // 2
    left, right = ring(rows, 1), ring(rows, -1)
    return [rows, right, left], [ring(left[:half], 1), ring(right[half:], -1)]


def across(blocks):
    return lax.all_to_all(blocks, "exp", split_axis=0, concat_axis=0, tiled=True)


def local(
    queries,
    key_heads,
    value_heads,
    residual,
    lengths,
    routes,
    gate_weights,
    out_weight,
    norm_gain,
    w_gate,
    w_up,
    w_down,
):
    columns = lax.axis_size("exp")
    token_count = residual.shape[1]
    model_width = residual.shape[2]

    routed = routes[0]
    node_count = routed.shape[1]
    capacity = max(2, 5 * token_count * node_count // (4 * columns))
    column = jnp.arange(columns, dtype=jnp.int32)
    slot = jnp.arange(capacity, dtype=jnp.int32)

    def slots_of(named):
        on_node = named[:, :, None] == column[None, None, :]
        member = jnp.sum(on_node.astype(jnp.int32), axis=1)
        before = jnp.cumsum(member, axis=0) - member
        return on_node, (before[:, :, None] == slot[None, None, :]) & (member[:, :, None] > 0)

    on_node, lookup = slots_of(routed)
    lookups = [slots_of(named)[1] for named in around(routed)]
    gate_pair = gate_weights[0].reshape(token_count, node_count, EXP_COL).astype(jnp.float32)
    node_route_gate = jnp.einsum(
        "tnc,tne->tce", on_node.astype(jnp.float32), gate_pair, precision=lax.Precision.HIGHEST
    )
    slot_gate = jnp.einsum(
        "qnr,qny->nyr",
        lookup.astype(jnp.float32),
        node_route_gate,
        precision=lax.Precision.HIGHEST,
    ).astype(jnp.bfloat16)
    gate_in = across(slot_gate.reshape(columns, EXP_COL * capacity))
    expert_pick = lax.axis_index("seq") // (lax.axis_size("seq") // EXP_COL)
    gates = [
        lax.dynamic_index_in_dim(
            g.reshape(columns, EXP_COL, capacity), expert_pick, axis=1, keepdims=False
        ).astype(jnp.float32)
        for g in around(gate_in)
    ]
    direct = capacity - SHARED_SLOTS
    part = jnp.arange(TILE_ROWS)
    shared_mask = (
        (
            lookup[:, :, :SHARED_SLOTS].transpose(1, 2, 0)[:, :, None, None, :]
            & (part[:, None] == part[None, :])[None, None, :, :, None]
        )
        .reshape(columns * SHARED_SLOTS * TILE_ROWS, TILE_ROWS * token_count)
        .astype(jnp.bfloat16)
    )
    ring_gates = [g[:, :SHARED_SLOTS].reshape(-1) for g in gates]
    near_gate = jnp.concatenate([ring_gates[i] for i in (0, 1, 3)])[:, None]
    far_gate = ring_gates[2][:, None]
    direct_gate = jnp.stack([g[:, SHARED_SLOTS:] for g in gates], axis=1).reshape(-1, 1)
    offset = jnp.arange(len(lookups))
    direct_masks = [
        (m[:, :, None, SHARED_SLOTS:] & (offset[None, None, :, None] == i))
        .reshape(token_count, -1)
        .astype(jnp.bfloat16)
        for i, m in enumerate(lookups)
    ]
    direct_mask = jnp.concatenate(direct_masks, axis=0)

    whole_q, whole_k, whole_v = (
        lax.all_to_all(queries[0], "seq", split_axis=1, concat_axis=0, tiled=True),
        lax.all_to_all(key_heads[0], "seq", split_axis=1, concat_axis=0, tiled=True),
        lax.all_to_all(value_heads[0], "seq", split_axis=1, concat_axis=0, tiled=True),
    )
    episode = episode_ids(lengths[0], whole_q.shape[0])
    mixed = attend(whole_q, whole_k, whole_v, episode)
    mixed, near_gate, far_gate, direct_gate, direct_mask, shared_mask = (
        lax.optimization_barrier(
            (mixed, near_gate, far_gate, direct_gate, direct_mask, shared_mask)
        )
    )
    turned = lax.dynamic_slice_in_dim(
        jnp.concatenate([mixed, mixed], axis=0),
        lax.axis_index("seq") * token_count,
        mixed.shape[0],
        axis=0,
    )
    head_partial = jnp.dot(
        turned,
        lax.all_gather(out_weight, "exp", axis=1, tiled=True),
        preferred_element_type=jnp.float32,
    ).astype(jnp.bfloat16)

    def by_owner(rows):
        return [rows[i : i + token_count] for i in range(0, rows.shape[0], token_count)]

    hidden = residual[0].astype(jnp.float32)
    for part in back_around(by_owner(head_partial)):
        hidden = hidden + part.astype(jnp.float32)
    inverse = lax.rsqrt(jnp.mean(hidden * hidden, axis=1, keepdims=True) + epsilon)
    normalized_rows = (hidden * inverse * norm_gain[None, :]).astype(jnp.bfloat16)

    gate_block, up_block, down_block = w_gate[0, 0], w_up[0, 0], w_down[0, 0]
    weights = (gate_block, up_block, down_block)
    shared_out = jnp.dot(
        shared_mask,
        normalized_rows.reshape(token_count, TILE_ROWS, -1).swapaxes(0, 1).reshape(
            TILE_ROWS * token_count, -1
        ),
        preferred_element_type=jnp.float32,
    ).astype(jnp.bfloat16)
    shared_in = across(shared_out.reshape(columns, -1, shared_out.shape[1])).reshape(-1, model_width)
    pack_rows = around(normalized_rows)
    near, far = gather_ring(shared_in)
    direct_out = jnp.einsum(
        "rq,rm->qm",
        direct_mask,
        jnp.concatenate(pack_rows, axis=0),
        preferred_element_type=jnp.float32,
    ).astype(jnp.bfloat16)
    direct_count = direct_out.shape[0]
    direct_rows = across(direct_out.reshape(columns, -1, model_width))
    block = shared_in.shape[0]
    seats = lax.axis_size("seq")
    parts = expert(
        near, near_gate, *weights, seats, ((0, 0, block), (1, block, block), (3, 2 * block, block))
    )
    parts = expert(far, far_gate, *weights, seats, ((2, 0, block),), into=parts)
    parts, direct_rows = lax.optimization_barrier((parts, direct_rows))
    direct_parts = expert(
        [direct_rows.reshape(direct_count, model_width)],
        direct_gate,
        *weights,
        1,
        ((0, 0, direct_count),),
    )
    direct_back = across(direct_parts.reshape(columns, -1, model_width))
    shared_sums = lax.psum_scatter(
        parts.reshape(-1, model_width), "seq", scatter_dimension=0, tiled=True
    )
    shared_back = across(shared_sums.reshape(columns, SHARED_SLOTS * TILE_ROWS, -1))
    pack_sums = jnp.einsum(
        "rq,qm->rm",
        direct_mask,
        direct_back.reshape(direct_count, model_width),
        preferred_element_type=jnp.float32,
    ).astype(jnp.bfloat16)
    shared_total = jnp.einsum(
        "qa,qc->ac",
        shared_mask,
        shared_back.reshape(shared_mask.shape[0], -1),
        preferred_element_type=jnp.float32,
    )
    total = hidden + shared_total.reshape(TILE_ROWS, token_count, -1).swapaxes(0, 1).reshape(
        token_count, model_width
    )
    for part in back_around(by_owner(pack_sums)):
        total = total + part.astype(jnp.float32)
    return total.astype(jnp.bfloat16)[None]


def solution(mesh):
    return jax.shard_map(
        local,
        mesh=mesh,
        in_specs=(
            P("exp", "seq", None),
            P("exp", "seq", None),
            P("exp", "seq", None),
            P("exp", "seq", None),
            P("exp", None),
            P("exp", "seq", None),
            P("exp", "seq", None),
            P("seq", "exp"),
            P(),
            P("exp", "seq", None, None),
            P("exp", "seq", None, None),
            P("exp", "seq", None, None),
        ),
        out_specs=P("exp", "seq", None),
        check_vma=False,
    )
```

time: 366 us -> 350 us (0.956)
  blocking collectives: 85.4 us -> 0 us
  waiting for transfers between devices: 127 us -> 168 us
  starting transfers between devices: 46.7 us -> 76.4 us
  local copies, waits for them, and re-layouts: 20.4 us -> 24.3 us
    ppermute x9 -> x19, waiting for transfers between devices: 7.11 us -> 95.9 us  [ring(): lax.ppermute(rows, 'seq', [(i, (i + step) % count) for i in range(count)])]
    all_to_all x2 -> x0, blocking collectives: 85.4 us -> none  [across(): lax.all_to_all(blocks, 'exp', split_axis=0, concat_axis=0, tiled=True)]
    all_to_all x3 -> x5, waiting for transfers between devices: 69.8 us -> 15.6 us  [across(): lax.all_to_all(blocks, 'exp', split_axis=0, concat_axis=0, tiled=True)]
    all_to_all x3 -> x5, starting transfers between devices: 23.6 us -> 39.5 us  [across(): lax.all_to_all(blocks, 'exp', split_axis=0, concat_axis=0, tiled=True)]
    ppermute x9 -> x19, starting transfers between devices: 12.5 us -> 26.6 us  [ring(): lax.ppermute(rows, 'seq', [(i, (i + step) % count) for i in range(count)])]
    reduce_scatter x3 -> x1, waiting for transfers between devices: 29.5 us -> 42.5 us  [local(): lax.psum_scatter(parts.reshape(-1, model_width), 'seq', scatter_dimension...]
    another operation x7 -> x1, local copies, waits for them, and re-layouts: 5.16 us -> 0.1 us  [local(): far_gate = ring_gates[2][:, None]]
    pallas_call x2 -> x3, Pallas kernels: 42.8 us -> 40.8 us  [expert(): pl.pallas_call(functools.partial(expert_kernel, sizes, places, aliased),...]
  transfers between devices with their start and end apart: 20 -> 29, of which waited for: 10 -> 16; matrix products, arithmetic and copies ran while one was open for 8% -> 10% of each run, Pallas kernels for 5% -> 12%
where the time goes in v1:
time: 350 us; the launch traced here: 349 us
  waiting for transfers between devices  168 us (48%)
  starting transfers between devices  76.4 us (22%)
  Pallas kernels  40.8 us (12%)
  local copies, waits for them, and re-layouts  24.3 us (7%)
  matrix products  19 us (5%)
  between operations  14.1 us (4%)
  other arithmetic  6.29 us (2%)
    ppermute x19, waiting for transfers between devices, ring(): lax.ppermute(rows, 'seq', [(i, (i + step) % count) for i in range(count)])  95.9 us
    reduce_scatter x1, waiting for transfers between devices, local(): lax.psum_scatter(parts.reshape(-1, model_width), 'seq', scatter_dimension...  42.5 us
    pallas_call x3, Pallas kernels, expert(): pl.pallas_call(functools.partial(expert_kernel, sizes, places, aliased),...  40.8 us
    all_to_all x5, starting transfers between devices, across(): lax.all_to_all(blocks, 'exp', split_axis=0, concat_axis=0, tiled=True)  39.5 us
    ppermute x19, starting transfers between devices, ring(): lax.ppermute(rows, 'seq', [(i, (i + step) % count) for i in range(count)])  26.6 us
    all_to_all x5, waiting for transfers between devices, across(): lax.all_to_all(blocks, 'exp', split_axis=0, concat_axis=0, tiled=True)  15.6 us
  transfers between devices with their start and end apart: 29, of which 16 were waited for; matrix products, arithmetic and copies ran while one was open for 10% of the time, Pallas kernels for 12%

profile of v1, /device:TPU:1, one launch (start us, length us, event | category | flops | bytes accessed | tf_op | source)
XLA Modules:
  0.0 349.0 jit_solution(1074784885585704734)
XLA Ops:
  9.8 3.3 collective-permute-start.4
  17.3 8.6 %all-to-all-start.3 = ((bf16[32,1,20]{2,1,0:T(2,128)(2,1)}), bf16[32,1,20]{2,1,0:T(2,128)(2,1)S(1)}, u32[]{:S(2)}, u32[]{:S(2)}) async-start(bf16[32,1,20]{2,1,0:T(2,128)(2,1)} %reshape.312), calls=%async_computation.3 | async-start | bytes 32768 | tf_op jit(solution)/shard_map/all_to_all | solution.py:186
  32.7 2.9 reshape.307
  37.5 3.5 all-to-all-start.1
  50.7 3.3 all-to-all-start
  54.6 3.8 %all-to-all-done = bf16[64,4,128]{2,0,1:T(8,128)(2,1)S(1)} async-done(((bf16[64,4,128]{2,0,1:T(8,128)(2,1)}), bf16[64,4,128]{2,0,1:T(8,128)(2,1)S(1)}, u32[]{:S(2)}, u32[]{:S(2)}) %all-to-all-start) | async-done | bytes 65568 | tf_op jit(solution)/shard_map/all_to_all | solution.py:264
  58.5 3.5 all-to-all-start.2
  62.7 3.5 %all-to-all-done.2 = bf16[64,4,128]{2,0,1:T(8,128)(2,1)S(1)} async-done(((bf16[64,4,128]{2,0,1:T(8,128)(2,1)}), bf16[64,4,128]{2,0,1:T(8,128)(2,1)S(1)}, u32[]{:S(2)}, u32[]{:S(2)}) %all-to-all-start.2) | async-done | bytes 65568 | tf_op jit(solution)/shard_map/all_to_all | solution.py:265
  66.8 6.0 %all-gather.2.cloned.1.call-done = bf16[1024,4096]{1,0:T(8,128)(2,1)} async-done(((bf16[1024,128]{1,0:T(8,128)(2,1)}), bf16[1024,4096]{1,0:T(8,128)(2,1)}) %all-gather.2.cloned.1.call-update) | async-done | bytes 8388624 | tf_op jit(solution)/shard_map/all_gather | solution.py:282
  72.8 6.0 %convolution_convert_fusion.1 = bf16[256,4096]{1,0:T(8,128)(2,1)S(1)} fusion(bf16[1024,4096]{1,0:T(8,128)(2,1)} %all-gather.2.cloned.1.call-done, s32[]{:T(128)S(6)} %select_n.22, bf16[256,1024]{0,1:T(8,128)(2,1)S(1)} %bitcast.131), kind=kOutput, calls=%fused_computation.2 | convolution fusion | flops 2149580800 | bytes 11010052 | tf_op jit(solution)/shard_map/dot_general | solution.py:280
  82.8 21.1 %collective-permute-done.8 = bf16[64,4096]{1,0:T(8,128)(2,1)S(1)} collective-permute-done((bf16[64,4096]{1,0:T(8,128)(2,1)S(1)}, bf16[64,4096]{1,0:T(8,128)(2,1)S(1)}, u32[]{:S(2)}, u32[]{:S(2)}) %collective-permute-start.8) | collective-permute-done | bytes 524320 | tf_op jit(solution)/shard_map/ppermute | solution.py:168
  103.9 4.4 %collective-permute-done.6 = bf16[64,4096]{1,0:T(8,128)(2,1)S(1)} collective-permute-done((bf16[64,4096]{1,0:T(8,128)(2,1)S(1)}, bf16[64,4096]{1,0:T(8,128)(2,1)S(1)}, u32[]{:S(2)}, u32[]{:S(2)}) %collective-permute-start.6) | collective-permute-done | bytes 524320 | tf_op jit(solution)/shard_map/ppermute | solution.py:168
  112.7 5.8 %all-to-all-start.4 = ((bf16[32,48,512]{2,1,0:T(8,128)(2,1)}), bf16[32,48,512]{2,1,0:T(8,128)(2,1)S(1)}, u32[]{:S(2)}, u32[]{:S(2)}) async-start(bf16[32,48,512]{2,1,0:T(8,128)(2,1)} %bitcast.129), calls=%async_computation.4 | async-start | bytes 3145728 | tf_op jit(solution)/shard_map/all_to_all | solution.py:186
  121.3 23.1 %collective-permute-done.15 = bf16[64,4096]{1,0:T(8,128)(2,1)S(1)} collective-permute-done((bf16[64,4096]{1,0:T(8,128)(2,1)S(1)}, bf16[64,4096]{1,0:T(8,128)(2,1)S(1)}, u32[]{:S(2)}, u32[]{:S(2)}) %collective-permute-start.15) | collective-permute-done | bytes 524320 | tf_op jit(solution)/shard_map/ppermute | solution.py:168
  144.7 2.9 convolution_convert_fusion
  147.6 8.4 %all-to-all-start.5 = ((bf16[32,16,4096]{2,1,0:T(8,128)(2,1)}), bf16[32,16,4096]{2,1,0:T(8,128)(2,1)}, u32[]{:S(2)}, u32[]{:S(2)}) async-start(bf16[32,16,4096]{2,1,0:T(8,128)(2,1)} %bitcast.123), calls=%async_computation.5 | async-start | bytes 8388608 | tf_op jit(solution)/shard_map/all_to_all | solution.py:186
  159.9 34.0 %collective-permute-done.9.refs_2_ = bf16[192,4096]{1,0:T(8,128)(2,1)} collective-permute-done((bf16[192,4096]{1,0:T(8,128)(2,1)S(1)}, bf16[192,4096]{1,0:T(8,128)(2,1)}, u32[]{:S(2)}, u32[]{:S(2)}) %collective-permute-start.9) | collective-permute-done | bytes 1572896 | tf_op jit(solution)/shard_map/ppermute | solution.py:168
  195.3 2.9 collective-permute-start.12
  198.2 16.6 %expert.3.refs_6_ = bf16[4,192,4096]{2,1,0:T(8,128)(2,1)} custom-call(bf16[192,4096]{1,0:T(8,128)(2,1)S(1)} %reshape.293.refs_0_, bf16[192,4096]{1,0:T(8,128)(2,1)S(1)} %collective-permute-done.11.refs_1_, bf16[192,4096]{1,0:T(8,128)(2,1)} %collective-permute-done.9.refs_2_, f32[576,1]{1,0:T(8,128)S(1)} %copy.272.refs_3_, bf16[4096,768]{1,0:T(8,128)(2,1)} %bitcast.113, ...), custom_call_target="tpu_custom_call" | custom-call | flops 10871635968 | bytes 28311552 | tf_op jit(solution)/shard_map/expert/pallas_call | solution.py:137
  214.8 9.0 %expert.4 = bf16[4,192,4096]{2,1,0:T(8,128)(2,1)} custom-call(bf16[96,4096]{1,0:T(8,128)(2,1)S(1)} %collective-permute-done.10.refs_0_, bf16[96,4096]{1,0:T(8,128)(2,1)S(1)} %collective-permute-done.12.refs_1_, f32[192,1]{1,0:T(8,128)S(1)} %copy.273.refs_2_, bf16[4096,768]{1,0:T(8,128)(2,1)} %bitcast.114, ...), custom_call_target="tpu_custom_call", output_to_operand_aliasing={{}: (6, {})} | custom-call | flops 3623878656 | bytes 22020096 | tf_op jit(solution)/shard_map/expert/pallas_call | solution.py:137
  224.0 15.3 %expert.5 = bf16[1,512,4096]{2,1,0:T(8,128)(2,1)} custom-call(bf16[512,4096]{1,0:T(8,128)(2,1)} %bitcast.50.refs_0_, f32[512,1]{1,0:T(8,128)S(1)} %copy.275.refs_1_, bf16[4096,768]{1,0:T(8,128)(2,1)} %bitcast.115, bf16[4096,768]{1,0:T(8,128)(2,1)} %bitcast.118, bf16[768,4096]{1,0:T(8,128)(2,1)} %bitcast.121), custom_call_target="tpu_custom_call" | custom-call | flops 9663676416 | bytes 27262976 | tf_op jit(solution)/shard_map/expert/pallas_call | solution.py:137
  239.3 8.8 %all-to-all-start.7 = ((bf16[32,16,4096]{2,1,0:T(8,128)(2,1)}), bf16[32,16,4096]{2,1,0:T(8,128)(2,1)}, u32[]{:S(2)}, u32[]{:S(2)}) async-start(bf16[32,16,4096]{2,1,0:T(8,128)(2,1)} %bitcast.124), calls=%async_computation.8 | async-start | bytes 8388608 | tf_op jit(solution)/shard_map/all_to_all | solution.py:186
  248.1 42.5 %reduce-scatter.2.cloned.1.call-done = bf16[192,4096]{1,0:T(8,128)(2,1)} async-done(((bf16[768,4096]{1,0:T(8,128)(2,1)}), bf16[192,4096]{1,0:T(8,128)(2,1)}) %reduce-scatter.2.cloned.1.call-update) | async-done | bytes 1572880 | tf_op jit(solution)/shard_map/reduce_scatter | solution.py:330
  290.6 3.8 %reshape.296 = bf16[32,48,512]{2,1,0:T(8,128)(2,1)} reshape(bf16[192,4096]{1,0:T(8,128)(2,1)} %reduce-scatter.2.cloned.1.call-done) | data formatting | bytes 3145728 | tf_op jit(solution)/shard_map/reshape | solution.py:333
  294.3 4.0 %all-to-all-done.7 = bf16[32,16,4096]{2,1,0:T(8,128)(2,1)} async-done(((bf16[32,16,4096]{2,1,0:T(8,128)(2,1)}), bf16[32,16,4096]{2,1,0:T(8,128)(2,1)}, u32[]{:S(2)}, u32[]{:S(2)}) %all-to-all-start.7) | async-done | bytes 4194336 | tf_op jit(solution)/shard_map/all_to_all | solution.py:186
  298.3 7.8 %all-to-all-start.6 = ((bf16[32,48,512]{2,1,0:T(8,128)(2,1)}), bf16[32,48,512]{2,1,0:T(8,128)(2,1)}, u32[]{:S(2)}, u32[]{:S(2)}) async-start(bf16[32,48,512]{2,1,0:T(8,128)(2,1)} %reshape.296), calls=%async_computation.7 | async-start | bytes 3145728 | tf_op jit(solution)/shard_map/all_to_all | solution.py:186
  306.2 3.5 convolution_convert_fusion.2
  310.8 2.8 collective-permute-start.18
  316.8 11.6 %all-to-all-done.6 = bf16[32,48,512]{2,1,0:T(8,128)(2,1)} async-done(((bf16[32,48,512]{2,1,0:T(8,128)(2,1)}), bf16[32,48,512]{2,1,0:T(8,128)(2,1)}, u32[]{:S(2)}, u32[]{:S(2)}) %all-to-all-start.6) | async-done | bytes 1572896 | tf_op jit(solution)/shard_map/all_to_all | solution.py:186
  328.4 2.9 convolution_bitcast_fusion
  331.4 4.5 %collective-permute-done.18 = bf16[64,4096]{1,0:T(8,128)(2,1)S(1)} collective-permute-done((bf16[64,4096]{1,0:T(8,128)(2,1)}, bf16[64,4096]{1,0:T(8,128)(2,1)S(1)}, u32[]{:S(2)}, u32[]{:S(2)}) %collective-permute-start.18) | collective-permute-done | bytes 524320 | tf_op jit(solution)/shard_map/ppermute | solution.py:168
  335.9 4.0 %collective-permute-done.16 = bf16[64,4096]{1,0:T(8,128)(2,1)} collective-permute-done((bf16[64,4096]{1,0:T(8,128)(2,1)}, bf16[64,4096]{1,0:T(8,128)(2,1)}, u32[]{:S(2)}, u32[]{:S(2)}) %collective-permute-start.16) | collective-permute-done | bytes 524320 | tf_op jit(solution)/shard_map/ppermute | solution.py:168
  (169 shorter events, 50.9 us)
Async XLA Ops:
  6.5 66.2 %all-gather.2.cloned.1.call-start = ((), (), s32[]{:S(2)}) async-start(), calls=%async_computation.9 | async-start | bytes 8650752 | tf_op jit(solution)/shard_map/all_gather | solution.py:282
  7.3 28.3 %collective-permute-start.5 = (s32[64,4]{0,1:T(4,128)}, s32[64,4]{0,1:T(4,128)S(1)}, u32[]{:S(2)}, u32[]{:S(2)}) collective-permute-start(s32[64,4]{0,1:T(4,128)} %bitcast.143), channel_id=1, source_target_pairs={{0,32},{32,64},{64,96},{96,0},{1,33},{33,65},{65,97},{97,1},{2,34}... | collective-permute-start | bytes 3080 | tf_op jit(solution)/shard_map/ppermute | solution.py:168
  9.8 25.8 %collective-permute-start.4 = (s32[64,4]{0,1:T(4,128)}, s32[64,4]{0,1:T(4,128)S(1)}, u32[]{:S(2)}, u32[]{:S(2)}) collective-permute-start(s32[64,4]{0,1:T(4,128)} %bitcast.144), channel_id=1, source_target_pairs={{0,64},{32,96},{64,0},{96,32},{1,65},{33,97},{65,1},{97,33},{2,66}... | collective-permute-start | bytes 3080 | tf_op jit(solution)/shard_map/ppermute | solution.py:168
  13.1 23.0 %collective-permute-start.3 = (s32[64,4]{0,1:T(4,128)}, s32[64,4]{0,1:T(4,128)S(1)}, u32[]{:S(2)}, u32[]{:S(2)}) collective-permute-start(s32[64,4]{0,1:T(4,128)} %bitcast.145), channel_id=1, source_target_pairs={{0,96},{32,0},{64,32},{96,64},{1,97},{33,1},{65,33},{97,65},{2,98}... | collective-permute-start | bytes 3080 | tf_op jit(solution)/shard_map/ppermute | solution.py:168
  17.3 20.3 %all-to-all-start.3 = ((bf16[32,1,20]{2,1,0:T(2,128)(2,1)}), bf16[32,1,20]{2,1,0:T(2,128)(2,1)S(1)}, u32[]{:S(2)}, u32[]{:S(2)}) async-start(bf16[32,1,20]{2,1,0:T(2,128)(2,1)} %reshape.312), calls=%async_computation.3 | async-start | bytes 32768 | tf_op jit(solution)/shard_map/all_to_all | solution.py:186
  37.5 107.2 %copy-start.3 = (bf16[256,512]{0,1:T(8,128)(2,1)}, bf16[256,512]{0,1:T(8,128)(2,1)S(1)}, u32[]{:S(2)}) copy-start(bf16[256,512]{0,1:T(8,128)(2,1)S(1)} %add_convert_fusion.1) | copy-start | bytes 786436
  37.5 13.2 %all-to-all-start.1 = ((bf16[64,4,1024]{2,0,1:T(8,128)(2,1)}), bf16[64,4,1024]{2,0,1:T(8,128)(2,1)S(1)}, u32[]{:S(2)}, u32[]{:S(2)}) async-start(bf16[64,4,1024]{2,0,1:T(8,128)(2,1)} %copy.242), calls=%async_computation.1 | async-start | bytes 1048576 | tf_op jit(solution)/shard_map/all_to_all | solution.py:263
  41.1 6.3 %collective-permute-start.1 = (bf16[32,20]{0,1:T(8,128)(2,1)S(1)}, bf16[32,20]{0,1:T(8,128)(2,1)S(1)}, u32[]{:S(2)}, u32[]{:S(2)}) collective-permute-start(bf16[32,20]{0,1:T(8,128)(2,1)S(1)} %bitcast.139), channel_id=1, source_target_pairs={{0,32},{32,64},{64,96},{96,0},{1,33},{33,65},{65,97},{97,1},{2,34}... | collective-permute-start | bytes 3848 | tf_op jit(solution)/shard_map/ppermute | solution.py:168
  42.6 6.5 %collective-permute-start = (bf16[32,20]{0,1:T(8,128)(2,1)S(1)}, bf16[32,20]{0,1:T(8,128)(2,1)S(1)}, u32[]{:S(2)}, u32[]{:S(2)}) collective-permute-start(bf16[32,20]{0,1:T(8,128)(2,1)S(1)} %bitcast.140), channel_id=1, source_target_pairs={{0,96},{32,0},{64,32},{96,64},{1,97},{33,1},{65,33},{97,65},{2,98}... | collective-permute-start | bytes 3848 | tf_op jit(solution)/shard_map/ppermute | solution.py:168
  43.9 6.8 %collective-permute-start.2 = (bf16[32,20]{0,1:T(8,128)(2,1)S(1)}, bf16[32,20]{0,1:T(8,128)(2,1)S(1)}, u32[]{:S(2)}, u32[]{:S(2)}) collective-permute-start(bf16[32,20]{0,1:T(8,128)(2,1)S(1)} %bitcast.141), channel_id=1, source_target_pairs={{0,64},{32,96},{64,0},{96,32},{1,65},{33,97},{65,1},{97,33},{2,66}... | collective-permute-start | bytes 3848 | tf_op jit(solution)/shard_map/ppermute | solution.py:168
  50.7 7.7 %all-to-all-start = ((bf16[64,4,128]{2,0,1:T(8,128)(2,1)}), bf16[64,4,128]{2,0,1:T(8,128)(2,1)S(1)}, u32[]{:S(2)}, u32[]{:S(2)}) async-start(bf16[64,4,128]{2,0,1:T(8,128)(2,1)} %copy.241), calls=%async_computation | async-start | bytes 131072 | tf_op jit(solution)/shard_map/all_to_all | solution.py:264
  58.5 7.8 %all-to-all-start.2 = ((bf16[64,4,128]{2,0,1:T(8,128)(2,1)}), bf16[64,4,128]{2,0,1:T(8,128)(2,1)S(1)}, u32[]{:S(2)}, u32[]{:S(2)}) async-start(bf16[64,4,128]{2,0,1:T(8,128)(2,1)} %copy.244), calls=%async_computation.2 | async-start | bytes 131072 | tf_op jit(solution)/shard_map/all_to_all | solution.py:265
  78.8 29.5 %copy-start.6 = (bf16[1,64,4096]{2,1,0:T(8,128)(2,1)S(1)}, bf16[1,64,4096]{2,1,0:T(8,128)(2,1)}, u32[]{:S(2)}) copy-start(bf16[1,64,4096]{2,1,0:T(8,128)(2,1)} %param.15) | copy-start | bytes 1572868
  78.9 29.8 %copy-start.7 = (f32[4096]{0:T(1024)S(1)}, f32[4096]{0:T(1024)}, u32[]{:S(2)}) copy-start(f32[4096]{0:T(1024)} %param.20) | copy-start | bytes 49156
  78.9 24.9 %collective-permute-start.8 = (bf16[64,4096]{1,0:T(8,128)(2,1)S(1)}, bf16[64,4096]{1,0:T(8,128)(2,1)S(1)}, u32[]{:S(2)}, u32[]{:S(2)}) collective-permute-start(bf16[64,4096]{1,0:T(8,128)(2,1)S(1)} %get-tuple-element.27), channel_id=1, source_target_pairs={{0,96},{32,0},{64,32},{96,64},{1,97},{33,1},{65,33},{97,65},{2,98}... | collective-permute-start | bytes 1572872 | tf_op jit(solution)/shard_map/ppermute | solution.py:168
  81.7 22.2 %collective-permute-start.7 = (bf16[64,4096]{1,0:T(8,128)(2,1)S(1)}, bf16[64,4096]{1,0:T(8,128)(2,1)S(1)}, u32[]{:S(2)}, u32[]{:S(2)}) collective-permute-start(bf16[64,4096]{1,0:T(8,128)(2,1)S(1)} %get-tuple-element.28), channel_id=1, source_target_pairs={{0,64},{32,96},{64,0},{96,32},{1,65},{33,97},{65,1},{97,33},{2,66}... | collective-permute-start | bytes 1572872 | tf_op jit(solution)/shard_map/ppermute | solution.py:168
  82.1 26.2 %collective-permute-start.6 = (bf16[64,4096]{1,0:T(8,128)(2,1)S(1)}, bf16[64,4096]{1,0:T(8,128)(2,1)S(1)}, u32[]{:S(2)}, u32[]{:S(2)}) collective-permute-start(bf16[64,4096]{1,0:T(8,128)(2,1)S(1)} %get-tuple-element.26), channel_id=1, source_target_pairs={{0,32},{32,64},{64,96},{96,0},{1,33},{33,65},{65,97},{97,1},{2,34}... | collective-permute-start | bytes 1572872 | tf_op jit(solution)/shard_map/ppermute | solution.py:168
  112.7 34.9 %all-to-all-start.4 = ((bf16[32,48,512]{2,1,0:T(8,128)(2,1)}), bf16[32,48,512]{2,1,0:T(8,128)(2,1)S(1)}, u32[]{:S(2)}, u32[]{:S(2)}) async-start(bf16[32,48,512]{2,1,0:T(8,128)(2,1)} %bitcast.129), calls=%async_computation.4 | async-start | bytes 3145728 | tf_op jit(solution)/shard_map/all_to_all | solution.py:186
  118.6 25.8 %collective-permute-start.15 = (bf16[64,4096]{1,0:T(8,128)(2,1)S(1)}, bf16[64,4096]{1,0:T(8,128)(2,1)S(1)}, u32[]{:S(2)}, u32[]{:S(2)}) collective-permute-start(bf16[64,4096]{1,0:T(8,128)(2,1)S(1)} %multiply_convert_fusion), channel_id=1, source_target_pairs={{0,32},{32,64},{64,96},{96,0},{1,33},{33,65},{65,97},{97,1},{2,34}... | collective-permute-start | bytes 1572872 | tf_op jit(solution)/shard_map/ppermute | solution.py:168
  118.7 25.7 %collective-permute-start.14 = (bf16[64,4096]{1,0:T(8,128)(2,1)S(1)}, bf16[64,4096]{1,0:T(8,128)(2,1)S(1)}, u32[]{:S(2)}, u32[]{:S(2)}) collective-permute-start(bf16[64,4096]{1,0:T(8,128)(2,1)S(1)} %multiply_convert_fusion), channel_id=1, source_target_pairs={{0,64},{32,96},{64,0},{96,32},{1,65},{33,97},{65,1},{97,33},{2,66}... | collective-permute-start | bytes 1572872 | tf_op jit(solution)/shard_map/ppermute | solution.py:168
  120.2 24.5 %collective-permute-start.13 = (bf16[64,4096]{1,0:T(8,128)(2,1)S(1)}, bf16[64,4096]{1,0:T(8,128)(2,1)S(1)}, u32[]{:S(2)}, u32[]{:S(2)}) collective-permute-start(bf16[64,4096]{1,0:T(8,128)(2,1)S(1)} %multiply_convert_fusion), channel_id=1, source_target_pairs={{0,96},{32,0},{64,32},{96,64},{1,97},{33,1},{65,33},{97,65},{2,98}... | collective-permute-start | bytes 1572872 | tf_op jit(solution)/shard_map/ppermute | solution.py:168
  147.6 76.2 %all-to-all-start.5 = ((bf16[32,16,4096]{2,1,0:T(8,128)(2,1)}), bf16[32,16,4096]{2,1,0:T(8,128)(2,1)}, u32[]{:S(2)}, u32[]{:S(2)}) async-start(bf16[32,16,4096]{2,1,0:T(8,128)(2,1)} %bitcast.123), calls=%async_computation.5 | async-start | bytes 8388608 | tf_op jit(solution)/shard_map/all_to_all | solution.py:186
  156.0 134.5 %reduce-scatter.2.cloned.1.call-start = ((), (), s32[]{:S(2)}) async-start(), calls=%async_computation.10 | async-start | bytes 7864320 | tf_op jit(solution)/shard_map/reduce_scatter | solution.py:330
  156.9 37.1 %collective-permute-start.9 = (bf16[192,4096]{1,0:T(8,128)(2,1)S(1)}, bf16[192,4096]{1,0:T(8,128)(2,1)}, u32[]{:S(2)}, u32[]{:S(2)}) collective-permute-start(bf16[192,4096]{1,0:T(8,128)(2,1)S(1)} %reshape.293.refs_0_), channel_id=1, source_target_pairs={{0,32},{32,64},{64,96},{96,0},{1,33},{33,65},{65,97},{97,1},{2,34}... | collective-permute-start | bytes 4718600 | tf_op jit(solution)/shard_map/ppermute | solution.py:168
  157.0 38.2 %collective-permute-start.11 = (bf16[192,4096]{1,0:T(8,128)(2,1)S(1)}, bf16[192,4096]{1,0:T(8,128)(2,1)S(1)}, u32[]{:S(2)}, u32[]{:S(2)}) collective-permute-start(bf16[192,4096]{1,0:T(8,128)(2,1)S(1)} %reshape.293.refs_0_), channel_id=1, source_target_pairs={{0,96},{32,0},{64,32},{96,64},{1,97},{33,1},{65,33},{97,65},{2,98}... | collective-permute-start | bytes 4718600 | tf_op jit(solution)/shard_map/ppermute | solution.py:168
  195.1 19.7 %collective-permute-start.10 = (bf16[96,4096]{1,0:T(8,128)(2,1)S(1)}, bf16[96,4096]{1,0:T(8,128)(2,1)S(1)}, u32[]{:S(2)}, u32[]{:S(2)}) collective-permute-start(bf16[96,4096]{1,0:T(8,128)(2,1)S(1)} %slice.106), channel_id=1, source_target_pairs={{0,32},{32,64},{64,96},{96,0},{1,33},{33,65},{65,97},{97,1},{2,34}... | collective-permute-start | bytes 2359304 | tf_op jit(solution)/shard_map/ppermute | solution.py:168
  195.3 19.5 %collective-permute-start.12 = (bf16[96,4096]{1,0:T(8,128)(2,1)S(1)}, bf16[96,4096]{1,0:T(8,128)(2,1)S(1)}, u32[]{:S(2)}, u32[]{:S(2)}) collective-permute-start(bf16[96,4096]{1,0:T(8,128)(2,1)S(1)} %slice.107), channel_id=1, source_target_pairs={{0,96},{32,0},{64,32},{96,64},{1,97},{33,1},{65,33},{97,65},{2,98}... | collective-permute-start | bytes 2359304 | tf_op jit(solution)/shard_map/ppermute | solution.py:168
  239.3 59.1 %all-to-all-start.7 = ((bf16[32,16,4096]{2,1,0:T(8,128)(2,1)}), bf16[32,16,4096]{2,1,0:T(8,128)(2,1)}, u32[]{:S(2)}, u32[]{:S(2)}) async-start(bf16[32,16,4096]{2,1,0:T(8,128)(2,1)} %bitcast.124), calls=%async_computation.8 | async-start | bytes 8388608 | tf_op jit(solution)/shard_map/all_to_all | solution.py:186
  298.3 30.1 %all-to-all-start.6 = ((bf16[32,48,512]{2,1,0:T(8,128)(2,1)}), bf16[32,48,512]{2,1,0:T(8,128)(2,1)}, u32[]{:S(2)}, u32[]{:S(2)}) async-start(bf16[32,48,512]{2,1,0:T(8,128)(2,1)} %reshape.296), calls=%async_computation.7 | async-start | bytes 3145728 | tf_op jit(solution)/shard_map/all_to_all | solution.py:186
  310.8 25.1 %collective-permute-start.18 = (bf16[64,4096]{1,0:T(8,128)(2,1)}, bf16[64,4096]{1,0:T(8,128)(2,1)S(1)}, u32[]{:S(2)}, u32[]{:S(2)}) collective-permute-start(bf16[64,4096]{1,0:T(8,128)(2,1)} %get-tuple-element.24), channel_id=1, source_target_pairs={{0,96},{32,0},{64,32},{96,64},{1,97},{33,1},{65,33},{97,65},{2,98}... | collective-permute-start | bytes 1572872 | tf_op jit(solution)/shard_map/ppermute | solution.py:168
  313.6 22.3 %collective-permute-start.17 = (bf16[64,4096]{1,0:T(8,128)(2,1)}, bf16[64,4096]{1,0:T(8,128)(2,1)S(1)}, u32[]{:S(2)}, u32[]{:S(2)}) collective-permute-start(bf16[64,4096]{1,0:T(8,128)(2,1)} %get-tuple-element.25), channel_id=1, source_target_pairs={{0,64},{32,96},{64,0},{96,32},{1,65},{33,97},{65,1},{97,33},{2,66}... | collective-permute-start | bytes 1572872 | tf_op jit(solution)/shard_map/ppermute | solution.py:168
  313.6 26.3 %collective-permute-start.16 = (bf16[64,4096]{1,0:T(8,128)(2,1)}, bf16[64,4096]{1,0:T(8,128)(2,1)}, u32[]{:S(2)}, u32[]{:S(2)}) collective-permute-start(bf16[64,4096]{1,0:T(8,128)(2,1)} %get-tuple-element.23), channel_id=1, source_target_pairs={{0,32},{32,64},{64,96},{96,0},{1,33},{33,65},{65,97},{97,1},{2,34}... | collective-permute-start | bytes 1572872 | tf_op jit(solution)/shard_map/ppermute | solution.py:168
  (6 other events, 72.2 us)
Sparse Core Ops, SparseCore 0:
  9.5 63.1 all-gather.1
  224.0 66.5 reduce-scatter.1

commit v2 on v1

--- a/solution.py
+++ b/solution.py
@@ -155,7 +155,7 @@
         input_output_aliases={len(pieces) + 4: 0} if aliased else {},
         compiler_params=pltpu.CompilerParams(vmem_limit_bytes=50 * 1024 * 1024),
         cost_estimate=pl.CostEstimate(
-            flops=6 * total * width * ff,
+            flops=60 * total * width * ff,
             transcendentals=total * ff,
             bytes_accessed=2 * (3 * width * ff + 2 * total * width),
         ),
@@ -277,18 +277,21 @@
         mixed.shape[0],
         axis=0,
     )
-    head_partial = jnp.dot(
-        turned,
-        lax.all_gather(out_weight, "exp", axis=1, tiled=True),
-        preferred_element_type=jnp.float32,
-    ).astype(jnp.bfloat16)
+    whole_weight = lax.all_gather(out_weight, "exp", axis=1, tiled=True)
 
     def by_owner(rows):
         return [rows[i : i + token_count] for i in range(0, rows.shape[0], token_count)]
 
-    hidden = residual[0].astype(jnp.float32)
-    for part in back_around(by_owner(head_partial)):
-        hidden = hidden + part.astype(jnp.float32)
+    sides, side = [], model_width // 2
+    for at in range(0, model_width, side):
+        head_partial = jnp.dot(
+            turned, whole_weight[:, at : at + side], preferred_element_type=jnp.float32
+        ).astype(jnp.bfloat16)
+        summed = residual[0, :, at : at + side].astype(jnp.float32)
+        for part in back_around(by_owner(head_partial)):
+            summed = summed + part.astype(jnp.float32)
+        sides.append(summed)
+    hidden = jnp.concatenate(sides, axis=1)
     inverse = lax.rsqrt(jnp.mean(hidden * hidden, axis=1, keepdims=True) + epsilon)
     normalized_rows = (hidden * inverse * norm_gain[None, :]).astype(jnp.bfloat16)
 
@@ -302,7 +305,7 @@
         preferred_element_type=jnp.float32,
     ).astype(jnp.bfloat16)
     shared_in = across(shared_out.reshape(columns, -1, shared_out.shape[1])).reshape(-1, model_width)
-    pack_rows = around(normalized_rows)
+    shared_in, pack_rows = lax.optimization_barrier((shared_in, around(normalized_rows)))
     near, far = gather_ring(shared_in)
     direct_out = jnp.einsum(
         "rq,rm->qm",

time: 350 us -> 341 us (0.974)
  waiting for transfers between devices: 168 us -> 149 us
  local copies, waits for them, and re-layouts: 24.3 us -> 28.7 us
    ppermute x19 -> x22, waiting for transfers between devices: 95.9 us -> 56.9 us  [ring(): lax.ppermute(rows, 'seq', [(i, (i + step) % count) for i in range(count)])]
    all_to_all x5, waiting for transfers between devices: 15.6 us -> 36.9 us  [across(): lax.all_to_all(blocks, 'exp', split_axis=0, concat_axis=0, tiled=True)]
    ppermute x19 -> x22, starting transfers between devices: 26.6 us -> 28.5 us  [ring(): lax.ppermute(rows, 'seq', [(i, (i + step) % count) for i in range(count)])]
  transfers between devices with their start and end apart: 29 -> 32, of which waited for: 16 -> 19; matrix products, arithmetic and copies ran while one was open for 10% -> 12% of each run, Pallas kernels for 12% -> 12%
where the time goes in v2:
time: 341 us; the launch traced here: 340 us
  waiting for transfers between devices  149 us (44%)
  starting transfers between devices  77.5 us (23%)
  Pallas kernels  40.7 us (12%)
  local copies, waits for them, and re-layouts  28.7 us (8%)
  matrix products  20.3 us (6%)
  between operations  14.2 us (4%)
  other arithmetic  9.5 us (3%)
    ppermute x22, waiting for transfers between devices, ring(): lax.ppermute(rows, 'seq', [(i, (i + step) % count) for i in range(count)])  56.9 us
    reduce_scatter x1, waiting for transfers between devices, local(): lax.psum_scatter(parts.reshape(-1, model_width), 'seq', scatter_dimension...  41.7 us
    pallas_call x3, Pallas kernels, expert(): pl.pallas_call(functools.partial(expert_kernel, sizes, places, aliased),...  40.7 us
    all_to_all x5, starting transfers between devices, across(): lax.all_to_all(blocks, 'exp', split_axis=0, concat_axis=0, tiled=True)  38.9 us
    all_to_all x5, waiting for transfers between devices, across(): lax.all_to_all(blocks, 'exp', split_axis=0, concat_axis=0, tiled=True)  36.9 us
    ppermute x22, starting transfers between devices, ring(): lax.ppermute(rows, 'seq', [(i, (i + step) % count) for i in range(count)])  28.5 us
  transfers between devices with their start and end apart: 32, of which 19 were waited for; matrix products, arithmetic and copies ran while one was open for 12% of the time, Pallas kernels for 12%

profile of v2, /device:TPU:1, one launch (start us, length us, event | category | flops | bytes accessed | tf_op | source)
XLA Modules:
  0.0 339.9 jit_solution(10712884536567029389)
XLA Ops:
  9.8 3.3 collective-permute-start.4
  17.3 8.6 %all-to-all-start.3 = ((bf16[32,1,20]{2,1,0:T(2,128)(2,1)}), bf16[32,1,20]{2,1,0:T(2,128)(2,1)S(1)}, u32[]{:S(2)}, u32[]{:S(2)}) async-start(bf16[32,1,20]{2,1,0:T(2,128)(2,1)} %reshape.324), calls=%async_computation.3 | async-start | bytes 32768 | tf_op jit(solution)/shard_map/all_to_all | solution.py:186
  38.2 3.5 %all-to-all-start.1 = ((bf16[64,4,1024]{2,0,1:T(8,128)(2,1)}), bf16[64,4,1024]{2,0,1:T(8,128)(2,1)S(1)}, u32[]{:S(2)}, u32[]{:S(2)}) async-start(bf16[64,4,1024]{2,0,1:T(8,128)(2,1)} %copy.248), calls=%async_computation.1 | async-start | bytes 1048576 | tf_op jit(solution)/shard_map/all_to_all | solution.py:263
  51.4 3.3 all-to-all-start
  55.3 3.9 %all-to-all-done = bf16[64,4,128]{2,0,1:T(8,128)(2,1)S(1)} async-done(((bf16[64,4,128]{2,0,1:T(8,128)(2,1)}), bf16[64,4,128]{2,0,1:T(8,128)(2,1)S(1)}, u32[]{:S(2)}, u32[]{:S(2)}) %all-to-all-start) | async-done | bytes 65568 | tf_op jit(solution)/shard_map/all_to_all | solution.py:264
  59.2 3.3 all-to-all-start.2
  63.3 3.7 %all-to-all-done.2 = bf16[64,4,128]{2,0,1:T(8,128)(2,1)S(1)} async-done(((bf16[64,4,128]{2,0,1:T(8,128)(2,1)}), bf16[64,4,128]{2,0,1:T(8,128)(2,1)S(1)}, u32[]{:S(2)}, u32[]{:S(2)}) %all-to-all-start.2) | async-done | bytes 65568 | tf_op jit(solution)/shard_map/all_to_all | solution.py:265
  67.5 5.3 %all-gather.2.cloned.1.call-done = bf16[1024,4096]{1,0:T(8,128)(2,1)} async-done(((bf16[1024,128]{1,0:T(8,128)(2,1)}), bf16[1024,4096]{1,0:T(8,128)(2,1)}) %all-gather.2.cloned.1.call-update) | async-done | bytes 8388624 | tf_op jit(solution)/shard_map/all_gather | solution.py:280
  72.8 3.8 %fusion.4 = bf16[256,2048]{1,0:T(8,128)(2,1)S(1)} fusion(bf16[1024,4096]{1,0:T(8,128)(2,1)} %all-gather.2.cloned.1.call-done, s32[]{:T(128)S(6)} %select_n.22, bf16[256,1024]{0,1:T(8,128)(2,1)S(1)} %bitcast.155), kind=kOutput, calls=%fused_computation.8 | convolution fusion | flops 1075314688 | bytes 5767172 | tf_op jit(solution)/shard_map/dot_general | solution.py:287
  86.9 3.8 %collective-permute-done.8 = bf16[64,2048]{1,0:T(8,128)(2,1)S(1)} collective-permute-done((bf16[64,2048]{1,0:T(8,128)(2,1)S(1)}, bf16[64,2048]{1,0:T(8,128)(2,1)S(1)}, u32[]{:S(2)}, u32[]{:S(2)}) %collective-permute-start.8) | collective-permute-done | bytes 262176 | tf_op jit(solution)/shard_map/ppermute | solution.py:168
  90.8 5.7 %collective-permute-done.6 = bf16[64,2048]{1,0:T(8,128)(2,1)S(1)} collective-permute-done((bf16[64,2048]{1,0:T(8,128)(2,1)}, bf16[64,2048]{1,0:T(8,128)(2,1)S(1)}, u32[]{:S(2)}, u32[]{:S(2)}) %collective-permute-start.6) | collective-permute-done | bytes 262176 | tf_op jit(solution)/shard_map/ppermute | solution.py:168
  96.5 5.9 %collective-permute-done.11 = bf16[64,2048]{1,0:T(8,128)(2,1)S(1)} collective-permute-done((bf16[64,2048]{1,0:T(8,128)(2,1)}, bf16[64,2048]{1,0:T(8,128)(2,1)S(1)}, u32[]{:S(2)}, u32[]{:S(2)}) %collective-permute-start.11) | collective-permute-done | bytes 262176 | tf_op jit(solution)/shard_map/ppermute | solution.py:168
  103.7 3.1 collective-permute-done.9
  112.7 6.0 %all-to-all-start.4 = ((bf16[32,48,512]{2,1,0:T(8,128)(2,1)}), bf16[32,48,512]{2,1,0:T(8,128)(2,1)S(1)}, u32[]{:S(2)}, u32[]{:S(2)}) async-start(bf16[32,48,512]{2,1,0:T(8,128)(2,1)} %bitcast.128), calls=%async_computation.4 | async-start | bytes 3145728 | tf_op jit(solution)/shard_map/all_to_all | solution.py:186
  121.1 19.7 %all-to-all-done.4 = bf16[32,48,512]{2,1,0:T(8,128)(2,1)S(1)} async-done(((bf16[32,48,512]{2,1,0:T(8,128)(2,1)}), bf16[32,48,512]{2,1,0:T(8,128)(2,1)S(1)}, u32[]{:S(2)}, u32[]{:S(2)}) %all-to-all-start.4) | async-done | bytes 1572896 | tf_op jit(solution)/shard_map/all_to_all | solution.py:186
  141.6 5.7 %collective-permute-done.14 = bf16[64,4096]{1,0:T(8,128)(2,1)} collective-permute-done((bf16[64,4096]{1,0:T(8,128)(2,1)}, bf16[64,4096]{1,0:T(8,128)(2,1)}, u32[]{:S(2)}, u32[]{:S(2)}) %collective-permute-start.14) | collective-permute-done | bytes 524320 | tf_op jit(solution)/shard_map/ppermute | solution.py:168
  151.2 4.9 %convolution_convert_fusion = bf16[512,4096]{1,0:T(8,128)(2,1)} fusion(bf16[256,512]{0,1:T(8,128)(2,1)} %add_convert_fusion.1, bf16[64,4096]{1,0:T(8,128)(2,1)} %collective-permute-done.14, bf16[64,4096]{1,0:T(8,128)(2,1)} %collective-permute-done.13, bf16[64,4096]{1,0:T(8,128)(2,1)} %collective-permute-done.12, bf16[64,4096]{1,0:T(8,128)(2,1)} %multiply_convert_fusion), kind=kOutput, calls=%fused_computation.1 | convolution fusion | flops 1084227584 | bytes 6553600 | tf_op jit(solution)/shard_map/rq,rm->qm/dot_general | solution.py:310
  156.1 8.1 %all-to-all-start.5 = ((bf16[32,16,4096]{2,1,0:T(8,128)(2,1)}), bf16[32,16,4096]{2,1,0:T(8,128)(2,1)}, u32[]{:S(2)}, u32[]{:S(2)}) async-start(bf16[32,16,4096]{2,1,0:T(8,128)(2,1)} %bitcast.121), calls=%async_computation.5 | async-start | bytes 8388608 | tf_op jit(solution)/shard_map/all_to_all | solution.py:186
  164.3 19.8 %collective-permute-done.15.refs_2_ = bf16[192,4096]{1,0:T(8,128)(2,1)} collective-permute-done((bf16[192,4096]{1,0:T(8,128)(2,1)S(1)}, bf16[192,4096]{1,0:T(8,128)(2,1)}, u32[]{:S(2)}, u32[]{:S(2)}) %collective-permute-start.15) | collective-permute-done | bytes 1572896 | tf_op jit(solution)/shard_map/ppermute | solution.py:168
  185.4 2.9 collective-permute-start.18
  188.4 16.6 %expert.3.refs_6_ = bf16[4,192,4096]{2,1,0:T(8,128)(2,1)} custom-call(bf16[192,4096]{1,0:T(8,128)(2,1)S(1)} %reshape.304.refs_0_, bf16[192,4096]{1,0:T(8,128)(2,1)S(1)} %collective-permute-done.17.refs_1_, bf16[192,4096]{1,0:T(8,128)(2,1)} %collective-permute-done.15.refs_2_, f32[576,1]{1,0:T(8,128)S(1)} %copy.279.refs_3_, bf16[4096,768]{1,0:T(8,128)(2,1)} %bitcast.145, ...), custom_call_target="tpu_custom_call" | custom-call | flops 108716359680 | bytes 28311552 | tf_op jit(solution)/shard_map/expert/pallas_call | solution.py:137
  205.0 8.9 %expert.4 = bf16[4,192,4096]{2,1,0:T(8,128)(2,1)} custom-call(bf16[96,4096]{1,0:T(8,128)(2,1)S(1)} %collective-permute-done.16.refs_0_, bf16[96,4096]{1,0:T(8,128)(2,1)S(1)} %collective-permute-done.18.refs_1_, f32[192,1]{1,0:T(8,128)S(1)} %copy.280.refs_2_, bf16[4096,768]{1,0:T(8,128)(2,1)} %bitcast.146, ...), custom_call_target="tpu_custom_call", output_to_operand_aliasing={{}: (6, {})} | custom-call | flops 36238786560 | bytes 22020096 | tf_op jit(solution)/shard_map/expert/pallas_call | solution.py:137
  215.4 15.2 %expert.5 = bf16[1,512,4096]{2,1,0:T(8,128)(2,1)} custom-call(bf16[512,4096]{1,0:T(8,128)(2,1)} %bitcast.51.refs_0_, f32[512,1]{1,0:T(8,128)S(1)} %copy-done, bf16[4096,768]{1,0:T(8,128)(2,1)} %bitcast.147, bf16[4096,768]{1,0:T(8,128)(2,1)} %bitcast.150, bf16[768,4096]{1,0:T(8,128)(2,1)} %bitcast.153), custom_call_target="tpu_custom_call" | custom-call | flops 96636764160 | bytes 27262976 | tf_op jit(solution)/shard_map/expert/pallas_call | solution.py:137
  230.7 8.4 %all-to-all-start.7 = ((bf16[32,16,4096]{2,1,0:T(8,128)(2,1)}), bf16[32,16,4096]{2,1,0:T(8,128)(2,1)}, u32[]{:S(2)}, u32[]{:S(2)}) async-start(bf16[32,16,4096]{2,1,0:T(8,128)(2,1)} %bitcast.122), calls=%async_computation.8 | async-start | bytes 8388608 | tf_op jit(solution)/shard_map/all_to_all | solution.py:186
  239.1 41.7 %reduce-scatter.2.cloned.1.call-done = bf16[192,4096]{1,0:T(8,128)(2,1)} async-done(((bf16[768,4096]{1,0:T(8,128)(2,1)}), bf16[192,4096]{1,0:T(8,128)(2,1)}) %reduce-scatter.2.cloned.1.call-update) | async-done | bytes 1572880 | tf_op jit(solution)/shard_map/reduce_scatter | solution.py:333
  280.8 3.8 %reshape.307 = bf16[32,48,512]{2,1,0:T(8,128)(2,1)} reshape(bf16[192,4096]{1,0:T(8,128)(2,1)} %reduce-scatter.2.cloned.1.call-done) | data formatting | bytes 3145728 | tf_op jit(solution)/shard_map/reshape | solution.py:336
  284.5 4.8 %all-to-all-done.7 = bf16[32,16,4096]{2,1,0:T(8,128)(2,1)} async-done(((bf16[32,16,4096]{2,1,0:T(8,128)(2,1)}), bf16[32,16,4096]{2,1,0:T(8,128)(2,1)}, u32[]{:S(2)}, u32[]{:S(2)}) %all-to-all-start.7) | async-done | bytes 4194336 | tf_op jit(solution)/shard_map/all_to_all | solution.py:186
  289.4 7.8 %all-to-all-start.6 = ((bf16[32,48,512]{2,1,0:T(8,128)(2,1)}), bf16[32,48,512]{2,1,0:T(8,128)(2,1)}, u32[]{:S(2)}, u32[]{:S(2)}) async-start(bf16[32,48,512]{2,1,0:T(8,128)(2,1)} %reshape.307), calls=%async_computation.7 | async-start | bytes 3145728 | tf_op jit(solution)/shard_map/all_to_all | solution.py:186
  297.2 3.5 %convolution_convert_fusion.1 = bf16[256,4096]{1,0:T(8,128)(2,1)S(1)} fusion(bf16[256,512]{0,1:T(8,128)(2,1)S(1)} %copy-done.6, bf16[512,4096]{1,0:T(8,128)(2,1)} %bitcast.53), kind=kOutput, calls=%fused_computation.2 | convolution fusion | flops 1074790400 | bytes 6553600 | tf_op jit(solution)/shard_map/rq,qm->rm/dot_general | solution.py:337
  307.7 11.8 %all-to-all-done.6 = bf16[32,48,512]{2,1,0:T(8,128)(2,1)} async-done(((bf16[32,48,512]{2,1,0:T(8,128)(2,1)}), bf16[32,48,512]{2,1,0:T(8,128)(2,1)}, u32[]{:S(2)}, u32[]{:S(2)}) %all-to-all-start.6) | async-done | bytes 1572896 | tf_op jit(solution)/shard_map/all_to_all | solution.py:186
  322.4 4.4 %collective-permute-done.21 = bf16[64,4096]{1,0:T(8,128)(2,1)S(1)} collective-permute-done((bf16[64,4096]{1,0:T(8,128)(2,1)}, bf16[64,4096]{1,0:T(8,128)(2,1)S(1)}, u32[]{:S(2)}, u32[]{:S(2)}) %collective-permute-start.21) | collective-permute-done | bytes 524320 | tf_op jit(solution)/shard_map/ppermute | solution.py:168
  326.8 4.0 %collective-permute-done.19 = bf16[64,4096]{1,0:T(8,128)(2,1)} collective-permute-done((bf16[64,4096]{1,0:T(8,128)(2,1)}, bf16[64,4096]{1,0:T(8,128)(2,1)}, u32[]{:S(2)}, u32[]{:S(2)}) %collective-permute-start.19) | collective-permute-done | bytes 524320 | tf_op jit(solution)/shard_map/ppermute | solution.py:168
  (193 shorter events, 70.6 us)
Async XLA Ops:
  6.5 66.2 %all-gather.2.cloned.1.call-start = ((), (), s32[]{:S(2)}) async-start(), calls=%async_computation.9 | async-start | bytes 8650752 | tf_op jit(solution)/shard_map/all_gather | solution.py:280
  7.3 28.3 %collective-permute-start.5 = (s32[64,4]{0,1:T(4,128)}, s32[64,4]{0,1:T(4,128)S(1)}, u32[]{:S(2)}, u32[]{:S(2)}) collective-permute-start(s32[64,4]{0,1:T(4,128)} %bitcast.141), channel_id=1, source_target_pairs={{0,32},{32,64},{64,96},{96,0},{1,33},{33,65},{65,97},{97,1},{2,34}... | collective-permute-start | bytes 3080 | tf_op jit(solution)/shard_map/ppermute | solution.py:168
  9.8 25.8 %collective-permute-start.4 = (s32[64,4]{0,1:T(4,128)}, s32[64,4]{0,1:T(4,128)S(1)}, u32[]{:S(2)}, u32[]{:S(2)}) collective-permute-start(s32[64,4]{0,1:T(4,128)} %bitcast.142), channel_id=1, source_target_pairs={{0,64},{32,96},{64,0},{96,32},{1,65},{33,97},{65,1},{97,33},{2,66}... | collective-permute-start | bytes 3080 | tf_op jit(solution)/shard_map/ppermute | solution.py:168
  13.1 23.0 %collective-permute-start.3 = (s32[64,4]{0,1:T(4,128)}, s32[64,4]{0,1:T(4,128)S(1)}, u32[]{:S(2)}, u32[]{:S(2)}) collective-permute-start(s32[64,4]{0,1:T(4,128)} %bitcast.143), channel_id=1, source_target_pairs={{0,96},{32,0},{64,32},{96,64},{1,97},{33,1},{65,33},{97,65},{2,98}... | collective-permute-start | bytes 3080 | tf_op jit(solution)/shard_map/ppermute | solution.py:168
  17.3 21.0 %all-to-all-start.3 = ((bf16[32,1,20]{2,1,0:T(2,128)(2,1)}), bf16[32,1,20]{2,1,0:T(2,128)(2,1)S(1)}, u32[]{:S(2)}, u32[]{:S(2)}) async-start(bf16[32,1,20]{2,1,0:T(2,128)(2,1)} %reshape.324), calls=%async_computation.3 | async-start | bytes 32768 | tf_op jit(solution)/shard_map/all_to_all | solution.py:186
  38.2 13.2 %all-to-all-start.1 = ((bf16[64,4,1024]{2,0,1:T(8,128)(2,1)}), bf16[64,4,1024]{2,0,1:T(8,128)(2,1)S(1)}, u32[]{:S(2)}, u32[]{:S(2)}) async-start(bf16[64,4,1024]{2,0,1:T(8,128)(2,1)} %copy.248), calls=%async_computation.1 | async-start | bytes 1048576 | tf_op jit(solution)/shard_map/all_to_all | solution.py:263
  41.8 6.3 %collective-permute-start.1 = (bf16[32,20]{0,1:T(8,128)(2,1)S(1)}, bf16[32,20]{0,1:T(8,128)(2,1)S(1)}, u32[]{:S(2)}, u32[]{:S(2)}) collective-permute-start(bf16[32,20]{0,1:T(8,128)(2,1)S(1)} %bitcast.137), channel_id=1, source_target_pairs={{0,32},{32,64},{64,96},{96,0},{1,33},{33,65},{65,97},{97,1},{2,34}... | collective-permute-start | bytes 3848 | tf_op jit(solution)/shard_map/ppermute | solution.py:168
  43.2 6.5 %collective-permute-start = (bf16[32,20]{0,1:T(8,128)(2,1)S(1)}, bf16[32,20]{0,1:T(8,128)(2,1)S(1)}, u32[]{:S(2)}, u32[]{:S(2)}) collective-permute-start(bf16[32,20]{0,1:T(8,128)(2,1)S(1)} %bitcast.138), channel_id=1, source_target_pairs={{0,96},{32,0},{64,32},{96,64},{1,97},{33,1},{65,33},{97,65},{2,98}... | collective-permute-start | bytes 3848 | tf_op jit(solution)/shard_map/ppermute | solution.py:168
  44.5 6.8 %collective-permute-start.2 = (bf16[32,20]{0,1:T(8,128)(2,1)S(1)}, bf16[32,20]{0,1:T(8,128)(2,1)S(1)}, u32[]{:S(2)}, u32[]{:S(2)}) collective-permute-start(bf16[32,20]{0,1:T(8,128)(2,1)S(1)} %bitcast.139), channel_id=1, source_target_pairs={{0,64},{32,96},{64,0},{96,32},{1,65},{33,97},{65,1},{97,33},{2,66}... | collective-permute-start | bytes 3848 | tf_op jit(solution)/shard_map/ppermute | solution.py:168
  51.4 7.8 %all-to-all-start = ((bf16[64,4,128]{2,0,1:T(8,128)(2,1)}), bf16[64,4,128]{2,0,1:T(8,128)(2,1)S(1)}, u32[]{:S(2)}, u32[]{:S(2)}) async-start(bf16[64,4,128]{2,0,1:T(8,128)(2,1)} %copy.247), calls=%async_computation | async-start | bytes 131072 | tf_op jit(solution)/shard_map/all_to_all | solution.py:264
  59.2 7.8 %all-to-all-start.2 = ((bf16[64,4,128]{2,0,1:T(8,128)(2,1)}), bf16[64,4,128]{2,0,1:T(8,128)(2,1)S(1)}, u32[]{:S(2)}, u32[]{:S(2)}) async-start(bf16[64,4,128]{2,0,1:T(8,128)(2,1)} %copy.250), calls=%async_computation.2 | async-start | bytes 131072 | tf_op jit(solution)/shard_map/all_to_all | solution.py:265
  77.4 13.3 %collective-permute-start.8 = (bf16[64,2048]{1,0:T(8,128)(2,1)S(1)}, bf16[64,2048]{1,0:T(8,128)(2,1)S(1)}, u32[]{:S(2)}, u32[]{:S(2)}) collective-permute-start(bf16[64,2048]{1,0:T(8,128)(2,1)S(1)} %get-tuple-element.35), channel_id=1, source_target_pairs={{0,96},{32,0},{64,32},{96,64},{1,97},{33,1},{65,33},{97,65},{2,98}... | collective-permute-start | bytes 786440 | tf_op jit(solution)/shard_map/ppermute | solution.py:168
  80.1 10.7 %collective-permute-start.7 = (bf16[64,2048]{1,0:T(8,128)(2,1)}, bf16[64,2048]{1,0:T(8,128)(2,1)S(1)}, u32[]{:S(2)}, u32[]{:S(2)}) collective-permute-start(bf16[64,2048]{1,0:T(8,128)(2,1)} %get-tuple-element.36), channel_id=1, source_target_pairs={{0,64},{32,96},{64,0},{96,32},{1,65},{33,97},{65,1},{97,33},{2,66}... | collective-permute-start | bytes 786440 | tf_op jit(solution)/shard_map/ppermute | solution.py:168
  80.5 16.0 %collective-permute-start.6 = (bf16[64,2048]{1,0:T(8,128)(2,1)}, bf16[64,2048]{1,0:T(8,128)(2,1)S(1)}, u32[]{:S(2)}, u32[]{:S(2)}) collective-permute-start(bf16[64,2048]{1,0:T(8,128)(2,1)} %get-tuple-element.34), channel_id=1, source_target_pairs={{0,32},{32,64},{64,96},{96,0},{1,33},{33,65},{65,97},{97,1},{2,34}... | collective-permute-start | bytes 786440 | tf_op jit(solution)/shard_map/ppermute | solution.py:168
  83.5 18.8 %collective-permute-start.11 = (bf16[64,2048]{1,0:T(8,128)(2,1)}, bf16[64,2048]{1,0:T(8,128)(2,1)S(1)}, u32[]{:S(2)}, u32[]{:S(2)}) collective-permute-start(bf16[64,2048]{1,0:T(8,128)(2,1)} %get-tuple-element.38), channel_id=1, source_target_pairs={{0,96},{32,0},{64,32},{96,64},{1,97},{33,1},{65,33},{97,65},{2,98}... | collective-permute-start | bytes 786440 | tf_op jit(solution)/shard_map/ppermute | solution.py:168
  85.6 16.8 %collective-permute-start.10 = (bf16[64,2048]{1,0:T(8,128)(2,1)}, bf16[64,2048]{1,0:T(8,128)(2,1)S(1)}, u32[]{:S(2)}, u32[]{:S(2)}) collective-permute-start(bf16[64,2048]{1,0:T(8,128)(2,1)} %get-tuple-element.39), channel_id=1, source_target_pairs={{0,64},{32,96},{64,0},{96,32},{1,65},{33,97},{65,1},{97,33},{2,66}... | collective-permute-start | bytes 786440 | tf_op jit(solution)/shard_map/ppermute | solution.py:168
  90.8 16.1 %collective-permute-start.9 = (bf16[64,2048]{1,0:T(8,128)(2,1)}, bf16[64,2048]{1,0:T(8,128)(2,1)}, u32[]{:S(2)}, u32[]{:S(2)}) collective-permute-start(bf16[64,2048]{1,0:T(8,128)(2,1)} %get-tuple-element.37), channel_id=1, source_target_pairs={{0,32},{32,64},{64,96},{96,0},{1,33},{33,65},{65,97},{97,1},{2,34}... | collective-permute-start | bytes 786440 | tf_op jit(solution)/shard_map/ppermute | solution.py:168
  112.7 28.2 %all-to-all-start.4 = ((bf16[32,48,512]{2,1,0:T(8,128)(2,1)}), bf16[32,48,512]{2,1,0:T(8,128)(2,1)S(1)}, u32[]{:S(2)}, u32[]{:S(2)}) async-start(bf16[32,48,512]{2,1,0:T(8,128)(2,1)} %bitcast.128), calls=%async_computation.4 | async-start | bytes 3145728 | tf_op jit(solution)/shard_map/all_to_all | solution.py:186
  119.6 22.0 %collective-permute-start.12 = (bf16[64,4096]{1,0:T(8,128)(2,1)}, bf16[64,4096]{1,0:T(8,128)(2,1)}, u32[]{:S(2)}, u32[]{:S(2)}) collective-permute-start(bf16[64,4096]{1,0:T(8,128)(2,1)} %multiply_convert_fusion), channel_id=1, source_target_pairs={{0,96},{32,0},{64,32},{96,64},{1,97},{33,1},{65,33},{97,65},{2,98}... | collective-permute-start | bytes 1572872 | tf_op jit(solution)/shard_map/ppermute | solution.py:168
  120.4 21.2 %collective-permute-start.13 = (bf16[64,4096]{1,0:T(8,128)(2,1)}, bf16[64,4096]{1,0:T(8,128)(2,1)}, u32[]{:S(2)}, u32[]{:S(2)}) collective-permute-start(bf16[64,4096]{1,0:T(8,128)(2,1)} %multiply_convert_fusion), channel_id=1, source_target_pairs={{0,64},{32,96},{64,0},{96,32},{1,65},{33,97},{65,1},{97,33},{2,66}... | collective-permute-start | bytes 1572872 | tf_op jit(solution)/shard_map/ppermute | solution.py:168
  120.4 26.9 %collective-permute-start.14 = (bf16[64,4096]{1,0:T(8,128)(2,1)}, bf16[64,4096]{1,0:T(8,128)(2,1)}, u32[]{:S(2)}, u32[]{:S(2)}) collective-permute-start(bf16[64,4096]{1,0:T(8,128)(2,1)} %multiply_convert_fusion), channel_id=1, source_target_pairs={{0,32},{32,64},{64,96},{96,0},{1,33},{33,65},{65,97},{97,1},{2,34}... | collective-permute-start | bytes 1572872 | tf_op jit(solution)/shard_map/ppermute | solution.py:168
  147.3 36.8 %collective-permute-start.15 = (bf16[192,4096]{1,0:T(8,128)(2,1)S(1)}, bf16[192,4096]{1,0:T(8,128)(2,1)}, u32[]{:S(2)}, u32[]{:S(2)}) collective-permute-start(bf16[192,4096]{1,0:T(8,128)(2,1)S(1)} %reshape.304.refs_0_), channel_id=1, source_target_pairs={{0,32},{32,64},{64,96},{96,0},{1,33},{33,65},{65,97},{97,1},{2,34}... | collective-permute-start | bytes 4718600 | tf_op jit(solution)/shard_map/ppermute | solution.py:168
  147.3 38.1 %collective-permute-start.17 = (bf16[192,4096]{1,0:T(8,128)(2,1)S(1)}, bf16[192,4096]{1,0:T(8,128)(2,1)S(1)}, u32[]{:S(2)}, u32[]{:S(2)}) collective-permute-start(bf16[192,4096]{1,0:T(8,128)(2,1)S(1)} %reshape.304.refs_0_), channel_id=1, source_target_pairs={{0,96},{32,0},{64,32},{96,64},{1,97},{33,1},{65,33},{97,65},{2,98}... | collective-permute-start | bytes 4718600 | tf_op jit(solution)/shard_map/ppermute | solution.py:168
  156.1 58.4 %all-to-all-start.5 = ((bf16[32,16,4096]{2,1,0:T(8,128)(2,1)}), bf16[32,16,4096]{2,1,0:T(8,128)(2,1)}, u32[]{:S(2)}, u32[]{:S(2)}) async-start(bf16[32,16,4096]{2,1,0:T(8,128)(2,1)} %bitcast.121), calls=%async_computation.5 | async-start | bytes 8388608 | tf_op jit(solution)/shard_map/all_to_all | solution.py:186
  164.2 116.6 %reduce-scatter.2.cloned.1.call-start = ((), (), s32[]{:S(2)}) async-start(), calls=%async_computation.10 | async-start | bytes 7864320 | tf_op jit(solution)/shard_map/reduce_scatter | solution.py:333
  185.3 19.7 %collective-permute-start.16 = (bf16[96,4096]{1,0:T(8,128)(2,1)S(1)}, bf16[96,4096]{1,0:T(8,128)(2,1)S(1)}, u32[]{:S(2)}, u32[]{:S(2)}) collective-permute-start(bf16[96,4096]{1,0:T(8,128)(2,1)S(1)} %slice.144), channel_id=1, source_target_pairs={{0,32},{32,64},{64,96},{96,0},{1,33},{33,65},{65,97},{97,1},{2,34}... | collective-permute-start | bytes 2359304 | tf_op jit(solution)/shard_map/ppermute | solution.py:168
  185.4 19.5 %collective-permute-start.18 = (bf16[96,4096]{1,0:T(8,128)(2,1)S(1)}, bf16[96,4096]{1,0:T(8,128)(2,1)S(1)}, u32[]{:S(2)}, u32[]{:S(2)}) collective-permute-start(bf16[96,4096]{1,0:T(8,128)(2,1)S(1)} %slice.145), channel_id=1, source_target_pairs={{0,96},{32,0},{64,32},{96,64},{1,97},{33,1},{65,33},{97,65},{2,98}... | collective-permute-start | bytes 2359304 | tf_op jit(solution)/shard_map/ppermute | solution.py:168
  230.7 58.7 %all-to-all-start.7 = ((bf16[32,16,4096]{2,1,0:T(8,128)(2,1)}), bf16[32,16,4096]{2,1,0:T(8,128)(2,1)}, u32[]{:S(2)}, u32[]{:S(2)}) async-start(bf16[32,16,4096]{2,1,0:T(8,128)(2,1)} %bitcast.122), calls=%async_computation.8 | async-start | bytes 8388608 | tf_op jit(solution)/shard_map/all_to_all | solution.py:186
  289.4 30.1 %all-to-all-start.6 = ((bf16[32,48,512]{2,1,0:T(8,128)(2,1)}), bf16[32,48,512]{2,1,0:T(8,128)(2,1)}, u32[]{:S(2)}, u32[]{:S(2)}) async-start(bf16[32,48,512]{2,1,0:T(8,128)(2,1)} %reshape.307), calls=%async_computation.7 | async-start | bytes 3145728 | tf_op jit(solution)/shard_map/all_to_all | solution.py:186
  301.9 24.9 %collective-permute-start.21 = (bf16[64,4096]{1,0:T(8,128)(2,1)}, bf16[64,4096]{1,0:T(8,128)(2,1)S(1)}, u32[]{:S(2)}, u32[]{:S(2)}) collective-permute-start(bf16[64,4096]{1,0:T(8,128)(2,1)} %get-tuple-element.32), channel_id=1, source_target_pairs={{0,96},{32,0},{64,32},{96,64},{1,97},{33,1},{65,33},{97,65},{2,98}... | collective-permute-start | bytes 1572872 | tf_op jit(solution)/shard_map/ppermute | solution.py:168
  304.5 22.3 %collective-permute-start.20 = (bf16[64,4096]{1,0:T(8,128)(2,1)}, bf16[64,4096]{1,0:T(8,128)(2,1)S(1)}, u32[]{:S(2)}, u32[]{:S(2)}) collective-permute-start(bf16[64,4096]{1,0:T(8,128)(2,1)} %get-tuple-element.33), channel_id=1, source_target_pairs={{0,64},{32,96},{64,0},{96,32},{1,65},{33,97},{65,1},{97,33},{2,66}... | collective-permute-start | bytes 1572872 | tf_op jit(solution)/shard_map/ppermute | solution.py:168
  304.5 26.3 %collective-permute-start.19 = (bf16[64,4096]{1,0:T(8,128)(2,1)}, bf16[64,4096]{1,0:T(8,128)(2,1)}, u32[]{:S(2)}, u32[]{:S(2)}) collective-permute-start(bf16[64,4096]{1,0:T(8,128)(2,1)} %get-tuple-element.31), channel_id=1, source_target_pairs={{0,32},{32,64},{64,96},{96,0},{1,33},{33,65},{65,97},{97,1},{2,34}... | collective-permute-start | bytes 1572872 | tf_op jit(solution)/shard_map/ppermute | solution.py:168
  (15 other events, 135.8 us)
Sparse Core Ops, SparseCore 0:
  9.5 63.1 all-gather.1
  214.6 66.1 reduce-scatter.1

commit v3 on v2

--- a/solution.py
+++ b/solution.py
@@ -42,7 +42,7 @@
 
 
 SHARED_SLOTS = 6
-TILE_ROWS = 8
+ROW_PIECES = 4
 
 
 CHUNK = 1024
@@ -163,6 +163,43 @@
     )(*pieces, gate, w_gate, w_up, w_down, *(() if into is None else (into,)))
 
 
+PROJECT_BLOCKS = 4
+
+
+def project_kernel(x_ref, w_ref, *out_refs):
+    depth = x_ref.shape[1]
+    w = jnp.concatenate([w_ref[pl.ds(i * depth, depth)] for i in range(PROJECT_BLOCKS)], axis=1)
+    y = jnp.dot(x_ref[...], w, preferred_element_type=jnp.float32).astype(jnp.bfloat16)
+    size = out_refs[0].shape[0]
+    for i, out in enumerate(out_refs):
+        out[...] = y[i * size : (i + 1) * size]
+
+
+def project(x, weight_blocks, first_column, column_count, rows_each):
+    rows, depth = x.shape
+    block = weight_blocks.shape[1]
+    step = PROJECT_BLOCKS * block
+    skip = first_column // step
+    owners = rows // rows_each
+    return pl.pallas_call(
+        project_kernel,
+        grid=(column_count // step,),
+        in_specs=[
+            pl.BlockSpec((rows, depth), lambda i: (0, 0)),
+            pl.BlockSpec((PROJECT_BLOCKS * depth, block), lambda i: (skip + i, 0)),
+        ],
+        out_specs=[pl.BlockSpec((rows_each, step), lambda i: (0, i))] * owners,
+        out_shape=[jax.ShapeDtypeStruct((rows_each, column_count), jnp.bfloat16)] * owners,
+        compiler_params=pltpu.CompilerParams(vmem_limit_bytes=32 * 1024 * 1024),
+        cost_estimate=pl.CostEstimate(
+            flops=2 * rows * depth * column_count,
+            transcendentals=0,
+            bytes_accessed=2 * (rows * depth + depth * column_count + rows * column_count),
+        ),
+        name="project",
+    )(x, weight_blocks)
+
+
 def ring(rows, step):
     count = lax.axis_size("seq")
     return lax.ppermute(rows, "seq", [(i, (i + step) % count) for i in range(count)])
@@ -237,13 +274,13 @@
         for g in around(gate_in)
     ]
     direct = capacity - SHARED_SLOTS
-    part = jnp.arange(TILE_ROWS)
+    part = jnp.arange(ROW_PIECES)
     shared_mask = (
         (
             lookup[:, :, :SHARED_SLOTS].transpose(1, 2, 0)[:, :, None, None, :]
             & (part[:, None] == part[None, :])[None, None, :, :, None]
         )
-        .reshape(columns * SHARED_SLOTS * TILE_ROWS, TILE_ROWS * token_count)
+        .reshape(columns * SHARED_SLOTS * ROW_PIECES, ROW_PIECES * token_count)
         .astype(jnp.bfloat16)
     )
     ring_gates = [g[:, :SHARED_SLOTS].reshape(-1) for g in gates]
@@ -277,18 +314,15 @@
         mixed.shape[0],
         axis=0,
     )
-    whole_weight = lax.all_gather(out_weight, "exp", axis=1, tiled=True)
+    whole_weight = lax.all_gather(out_weight, "exp", axis=0, tiled=True)
 
     def by_owner(rows):
         return [rows[i : i + token_count] for i in range(0, rows.shape[0], token_count)]
 
     sides, side = [], model_width // 2
     for at in range(0, model_width, side):
-        head_partial = jnp.dot(
-            turned, whole_weight[:, at : at + side], preferred_element_type=jnp.float32
-        ).astype(jnp.bfloat16)
         summed = residual[0, :, at : at + side].astype(jnp.float32)
-        for part in back_around(by_owner(head_partial)):
+        for part in back_around(project(turned, whole_weight, at, side, token_count)):
             summed = summed + part.astype(jnp.float32)
         sides.append(summed)
     hidden = jnp.concatenate(sides, axis=1)
@@ -299,8 +333,8 @@
     weights = (gate_block, up_block, down_block)
     shared_out = jnp.dot(
         shared_mask,
-        normalized_rows.reshape(token_count, TILE_ROWS, -1).swapaxes(0, 1).reshape(
-            TILE_ROWS * token_count, -1
+        normalized_rows.reshape(token_count, ROW_PIECES, -1).swapaxes(0, 1).reshape(
+            ROW_PIECES * token_count, -1
         ),
         preferred_element_type=jnp.float32,
     ).astype(jnp.bfloat16)
@@ -333,7 +367,7 @@
     shared_sums = lax.psum_scatter(
         parts.reshape(-1, model_width), "seq", scatter_dimension=0, tiled=True
     )
-    shared_back = across(shared_sums.reshape(columns, SHARED_SLOTS * TILE_ROWS, -1))
+    shared_back = across(shared_sums.reshape(columns, SHARED_SLOTS * ROW_PIECES, -1))
     pack_sums = jnp.einsum(
         "rq,qm->rm",
         direct_mask,
@@ -346,7 +380,7 @@
         shared_back.reshape(shared_mask.shape[0], -1),
         preferred_element_type=jnp.float32,
     )
-    total = hidden + shared_total.reshape(TILE_ROWS, token_count, -1).swapaxes(0, 1).reshape(
+    total = hidden + shared_total.reshape(ROW_PIECES, token_count, -1).swapaxes(0, 1).reshape(
         token_count, model_width
     )
     for part in back_around(by_owner(pack_sums)):

time: 341 us -> 333 us (0.977)
  matrix products: 20.3 us -> 14.7 us
  waiting for transfers between devices: 149 us -> 145 us
  Pallas kernels: 40.7 us -> 44.5 us
    dot_general x3 -> x1, matrix products: 7.44 us -> 1.76 us  [local(): jnp.dot(shared_mask, normalized_rows.reshape(token_count, ROW_PIECES, -1)...]
    all_gather x1, waiting for transfers between devices: 5.27 us -> 0.51 us  [local(): whole_weight = lax.all_gather(out_weight, 'exp', axis=0, tiled=True)]
    pallas_call x0 -> x2, Pallas kernels: none -> 3.73 us  [project(): pl.pallas_call(project_kernel, grid=(column_count // step,), in_specs=[pl...]
  transfers between devices with their start and end apart: 32 -> 32, of which waited for: 19 -> 21; matrix products, arithmetic and copies ran while one was open for 12% -> 11% of each run, Pallas kernels for 12% -> 13%
where the time goes in v3:
time: 333 us; the launch traced here: 332 us
  waiting for transfers between devices  145 us (44%)
  starting transfers between devices  77.7 us (23%)
  Pallas kernels  44.5 us (13%)
  local copies, waits for them, and re-layouts  26 us (8%)
  matrix products  14.7 us (4%)
  between operations  14.2 us (4%)
  other arithmetic  9.89 us (3%)
    ppermute x22, waiting for transfers between devices, ring(): lax.ppermute(rows, 'seq', [(i, (i + step) % count) for i in range(count)])  57.9 us
    reduce_scatter x1, waiting for transfers between devices, local(): lax.psum_scatter(parts.reshape(-1, model_width), 'seq', scatter_dimension...  41.6 us
    pallas_call x3, Pallas kernels, expert(): pl.pallas_call(functools.partial(expert_kernel, sizes, places, aliased),...  40.8 us
    all_to_all x5, waiting for transfers between devices, across(): lax.all_to_all(blocks, 'exp', split_axis=0, concat_axis=0, tiled=True)  39.4 us
    all_to_all x5, starting transfers between devices, across(): lax.all_to_all(blocks, 'exp', split_axis=0, concat_axis=0, tiled=True)  38.8 us
    ppermute x22, starting transfers between devices, ring(): lax.ppermute(rows, 'seq', [(i, (i + step) % count) for i in range(count)])  28.8 us
  transfers between devices with their start and end apart: 32, of which 21 were waited for; matrix products, arithmetic and copies ran while one was open for 11% of the time, Pallas kernels for 13%

profile of v3, /device:TPU:1, one launch (start us, length us, event | category | flops | bytes accessed | tf_op | source)
XLA Modules:
  0.0 332.0 jit_solution(6304621742084496938)
XLA Ops:
  7.3 2.5 collective-permute-start.5
  9.8 3.3 collective-permute-start.4
  17.3 8.6 %all-to-all-start.3 = ((bf16[32,1,20]{2,1,0:T(2,128)(2,1)}), bf16[32,1,20]{2,1,0:T(2,128)(2,1)S(1)}, u32[]{:S(2)}, u32[]{:S(2)}) async-start(bf16[32,1,20]{2,1,0:T(2,128)(2,1)} %reshape.324), calls=%async_computation.3 | async-start | bytes 32768 | tf_op jit(solution)/shard_map/all_to_all | solution.py:223
  35.8 3.5 %all-to-all-start.1 = ((bf16[64,4,1024]{2,0,1:T(8,128)(2,1)}), bf16[64,4,1024]{2,0,1:T(8,128)(2,1)S(1)}, u32[]{:S(2)}, u32[]{:S(2)}) async-start(bf16[64,4,1024]{2,0,1:T(8,128)(2,1)} %copy.255), calls=%async_computation.1 | async-start | bytes 1048576 | tf_op jit(solution)/shard_map/all_to_all | solution.py:300
  49.0 3.3 all-to-all-start
  56.8 3.3 all-to-all-start.2
  61.7 2.8 all-to-all-done.2
  66.3 3.4 %copy-done = bf16[32768,128]{1,0:T(8,128)(2,1)S(1)} copy-done((bf16[32768,128]{1,0:T(8,128)(2,1)S(1)}, bf16[32768,128]{1,0:T(8,128)(2,1)}, u32[]{:S(2)}) %copy-start) | copy-done | bytes 8388632
  71.6 2.7 collective-permute-start.8
  82.4 9.0 %collective-permute-done.6 = bf16[64,2048]{1,0:T(8,128)(2,1)} collective-permute-done((bf16[64,2048]{1,0:T(8,128)(2,1)S(1)}, bf16[64,2048]{1,0:T(8,128)(2,1)}, u32[]{:S(2)}, u32[]{:S(2)}) %collective-permute-start.6) | collective-permute-done | bytes 262176 | tf_op jit(solution)/shard_map/ppermute | solution.py:205
  93.6 7.3 %collective-permute-done.9 = bf16[64,2048]{1,0:T(8,128)(2,1)} collective-permute-done((bf16[64,2048]{1,0:T(8,128)(2,1)S(1)}, bf16[64,2048]{1,0:T(8,128)(2,1)}, u32[]{:S(2)}, u32[]{:S(2)}) %collective-permute-start.9) | collective-permute-done | bytes 262176 | tf_op jit(solution)/shard_map/ppermute | solution.py:205
  105.1 5.8 %all-to-all-start.4 = ((bf16[32,24,1024]{2,1,0:T(8,128)(2,1)}), bf16[32,24,1024]{2,1,0:T(8,128)(2,1)S(1)}, u32[]{:S(2)}, u32[]{:S(2)}) async-start(bf16[32,24,1024]{2,1,0:T(8,128)(2,1)} %bitcast.118), calls=%async_computation.4 | async-start | bytes 3145728 | tf_op jit(solution)/shard_map/all_to_all | solution.py:223
  113.4 19.7 %all-to-all-done.4 = bf16[32,24,1024]{2,1,0:T(8,128)(2,1)S(1)} async-done(((bf16[32,24,1024]{2,1,0:T(8,128)(2,1)}), bf16[32,24,1024]{2,1,0:T(8,128)(2,1)S(1)}, u32[]{:S(2)}, u32[]{:S(2)}) %all-to-all-start.4) | async-done | bytes 1572896 | tf_op jit(solution)/shard_map/all_to_all | solution.py:223
  134.2 5.0 %collective-permute-done.14 = bf16[64,4096]{1,0:T(8,128)(2,1)} collective-permute-done((bf16[64,4096]{1,0:T(8,128)(2,1)}, bf16[64,4096]{1,0:T(8,128)(2,1)}, u32[]{:S(2)}, u32[]{:S(2)}) %collective-permute-start.14) | collective-permute-done | bytes 524320 | tf_op jit(solution)/shard_map/ppermute | solution.py:205
  139.2 2.7 collective-permute-start.17
  143.0 4.9 %convolution_convert_fusion = bf16[512,4096]{1,0:T(8,128)(2,1)} fusion(bf16[256,512]{0,1:T(8,128)(2,1)} %add_convert_fusion.1, bf16[64,4096]{1,0:T(8,128)(2,1)} %collective-permute-done.14, bf16[64,4096]{1,0:T(8,128)(2,1)} %collective-permute-done.13, bf16[64,4096]{1,0:T(8,128)(2,1)} %collective-permute-done.12, bf16[64,4096]{1,0:T(8,128)(2,1)} %multiply_convert_fusion), kind=kOutput, calls=%fused_computation | convolution fusion | flops 1084227584 | bytes 6553600 | tf_op jit(solution)/shard_map/rq,rm->qm/dot_general | solution.py:344
  147.9 8.1 %all-to-all-start.5 = ((bf16[32,16,4096]{2,1,0:T(8,128)(2,1)}), bf16[32,16,4096]{2,1,0:T(8,128)(2,1)}, u32[]{:S(2)}, u32[]{:S(2)}) async-start(bf16[32,16,4096]{2,1,0:T(8,128)(2,1)} %bitcast.119), calls=%async_computation.5 | async-start | bytes 8388608 | tf_op jit(solution)/shard_map/all_to_all | solution.py:223
  156.1 19.9 %collective-permute-done.15.refs_2_ = bf16[192,4096]{1,0:T(8,128)(2,1)} collective-permute-done((bf16[192,4096]{1,0:T(8,128)(2,1)S(1)}, bf16[192,4096]{1,0:T(8,128)(2,1)}, u32[]{:S(2)}, u32[]{:S(2)}) %collective-permute-start.15) | collective-permute-done | bytes 1572896 | tf_op jit(solution)/shard_map/ppermute | solution.py:205
  177.3 2.9 collective-permute-start.18
  180.3 16.6 %expert.3.refs_6_ = bf16[4,192,4096]{2,1,0:T(8,128)(2,1)} custom-call(bf16[192,4096]{1,0:T(8,128)(2,1)S(1)} %reshape.304.refs_0_, bf16[192,4096]{1,0:T(8,128)(2,1)S(1)} %collective-permute-done.17.refs_1_, bf16[192,4096]{1,0:T(8,128)(2,1)} %collective-permute-done.15.refs_2_, f32[576,1]{1,0:T(8,128)S(1)} %copy.287.refs_3_, bf16[4096,768]{1,0:T(8,128)(2,1)} %bitcast.144, ...), custom_call_target="tpu_custom_call" | custom-call | flops 108716359680 | bytes 28311552 | tf_op jit(solution)/shard_map/expert/pallas_call | solution.py:137
  196.9 8.9 %expert.4 = bf16[4,192,4096]{2,1,0:T(8,128)(2,1)} custom-call(bf16[96,4096]{1,0:T(8,128)(2,1)S(1)} %collective-permute-done.16.refs_0_, bf16[96,4096]{1,0:T(8,128)(2,1)S(1)} %collective-permute-done.18.refs_1_, f32[192,1]{1,0:T(8,128)S(1)} %copy.288.refs_2_, bf16[4096,768]{1,0:T(8,128)(2,1)} %bitcast.145, ...), custom_call_target="tpu_custom_call", output_to_operand_aliasing={{}: (6, {})} | custom-call | flops 36238786560 | bytes 22020096 | tf_op jit(solution)/shard_map/expert/pallas_call | solution.py:137
  207.3 15.3 %expert.5 = bf16[1,512,4096]{2,1,0:T(8,128)(2,1)} custom-call(bf16[512,4096]{1,0:T(8,128)(2,1)} %bitcast.51.refs_0_, f32[512,1]{1,0:T(8,128)S(1)} %copy-done.1, bf16[4096,768]{1,0:T(8,128)(2,1)} %bitcast.146, bf16[4096,768]{1,0:T(8,128)(2,1)} %bitcast.149, bf16[768,4096]{1,0:T(8,128)(2,1)} %bitcast.152), custom_call_target="tpu_custom_call" | custom-call | flops 96636764160 | bytes 27262976 | tf_op jit(solution)/shard_map/expert/pallas_call | solution.py:137
  222.6 8.5 %all-to-all-start.7 = ((bf16[32,16,4096]{2,1,0:T(8,128)(2,1)}), bf16[32,16,4096]{2,1,0:T(8,128)(2,1)}, u32[]{:S(2)}, u32[]{:S(2)}) async-start(bf16[32,16,4096]{2,1,0:T(8,128)(2,1)} %bitcast.120), calls=%async_computation.8 | async-start | bytes 8388608 | tf_op jit(solution)/shard_map/all_to_all | solution.py:223
  231.1 41.6 %reduce-scatter.2.cloned.1.call-done = bf16[192,4096]{1,0:T(8,128)(2,1)} async-done(((bf16[768,4096]{1,0:T(8,128)(2,1)}), bf16[192,4096]{1,0:T(8,128)(2,1)}) %reduce-scatter.2.cloned.1.call-update) | async-done | bytes 1572880 | tf_op jit(solution)/shard_map/reduce_scatter | solution.py:367
  272.7 3.7 %reshape.307 = bf16[32,24,1024]{2,1,0:T(8,128)(2,1)} reshape(bf16[192,4096]{1,0:T(8,128)(2,1)} %reduce-scatter.2.cloned.1.call-done) | data formatting | bytes 3145728 | tf_op jit(solution)/shard_map/reshape | solution.py:370
  276.4 4.9 %all-to-all-done.7 = bf16[32,16,4096]{2,1,0:T(8,128)(2,1)} async-done(((bf16[32,16,4096]{2,1,0:T(8,128)(2,1)}), bf16[32,16,4096]{2,1,0:T(8,128)(2,1)}, u32[]{:S(2)}, u32[]{:S(2)}) %all-to-all-start.7) | async-done | bytes 4194336 | tf_op jit(solution)/shard_map/all_to_all | solution.py:223
  281.3 7.8 %all-to-all-start.6 = ((bf16[32,24,1024]{2,1,0:T(8,128)(2,1)}), bf16[32,24,1024]{2,1,0:T(8,128)(2,1)}, u32[]{:S(2)}, u32[]{:S(2)}) async-start(bf16[32,24,1024]{2,1,0:T(8,128)(2,1)} %reshape.307), calls=%async_computation.7 | async-start | bytes 3145728 | tf_op jit(solution)/shard_map/all_to_all | solution.py:223
  289.2 3.5 %convolution_convert_fusion.1 = bf16[256,4096]{1,0:T(8,128)(2,1)S(1)} fusion(bf16[256,512]{0,1:T(8,128)(2,1)S(1)} %copy-done.8, bf16[512,4096]{1,0:T(8,128)(2,1)} %bitcast.53), kind=kOutput, calls=%fused_computation.1 | convolution fusion | flops 1074790400 | bytes 6553600 | tf_op jit(solution)/shard_map/rq,qm->rm/dot_general | solution.py:371
  293.8 2.6 collective-permute-start.21
  297.2 14.2 %all-to-all-done.6 = bf16[32,24,1024]{2,1,0:T(8,128)(2,1)} async-done(((bf16[32,24,1024]{2,1,0:T(8,128)(2,1)}), bf16[32,24,1024]{2,1,0:T(8,128)(2,1)}, u32[]{:S(2)}, u32[]{:S(2)}) %all-to-all-start.6) | async-done | bytes 1572896 | tf_op jit(solution)/shard_map/all_to_all | solution.py:223
  313.6 5.2 %collective-permute-done.21 = bf16[64,4096]{1,0:T(8,128)(2,1)S(1)} collective-permute-done((bf16[64,4096]{1,0:T(8,128)(2,1)}, bf16[64,4096]{1,0:T(8,128)(2,1)S(1)}, u32[]{:S(2)}, u32[]{:S(2)}) %collective-permute-start.21) | collective-permute-done | bytes 524320 | tf_op jit(solution)/shard_map/ppermute | solution.py:205
  318.8 4.0 %collective-permute-done.19 = bf16[64,4096]{1,0:T(8,128)(2,1)} collective-permute-done((bf16[64,4096]{1,0:T(8,128)(2,1)}, bf16[64,4096]{1,0:T(8,128)(2,1)}, u32[]{:S(2)}, u32[]{:S(2)}) %collective-permute-start.19) | collective-permute-done | bytes 524320 | tf_op jit(solution)/shard_map/ppermute | solution.py:205
  (199 shorter events, 62.2 us)
Async XLA Ops:
  6.5 59.8 %all-gather.2.cloned.1.call-start = ((), (), s32[]{:S(2)}) async-start(), calls=%async_computation.9 | async-start | bytes 8650752 | tf_op jit(solution)/shard_map/all_gather | solution.py:317
  7.3 25.9 %collective-permute-start.5 = (s32[64,4]{0,1:T(4,128)}, s32[64,4]{0,1:T(4,128)S(1)}, u32[]{:S(2)}, u32[]{:S(2)}) collective-permute-start(s32[64,4]{0,1:T(4,128)} %bitcast.140), channel_id=1, source_target_pairs={{0,32},{32,64},{64,96},{96,0},{1,33},{33,65},{65,97},{97,1},{2,34}... | collective-permute-start | bytes 3080 | tf_op jit(solution)/shard_map/ppermute | solution.py:205
  9.8 23.4 %collective-permute-start.4 = (s32[64,4]{0,1:T(4,128)}, s32[64,4]{0,1:T(4,128)S(1)}, u32[]{:S(2)}, u32[]{:S(2)}) collective-permute-start(s32[64,4]{0,1:T(4,128)} %bitcast.141), channel_id=1, source_target_pairs={{0,64},{32,96},{64,0},{96,32},{1,65},{33,97},{65,1},{97,33},{2,66}... | collective-permute-start | bytes 3080 | tf_op jit(solution)/shard_map/ppermute | solution.py:205
  13.1 20.6 %collective-permute-start.3 = (s32[64,4]{0,1:T(4,128)}, s32[64,4]{0,1:T(4,128)S(1)}, u32[]{:S(2)}, u32[]{:S(2)}) collective-permute-start(s32[64,4]{0,1:T(4,128)} %bitcast.142), channel_id=1, source_target_pairs={{0,96},{32,0},{64,32},{96,64},{1,97},{33,1},{65,33},{97,65},{2,98}... | collective-permute-start | bytes 3080 | tf_op jit(solution)/shard_map/ppermute | solution.py:205
  17.3 18.5 %all-to-all-start.3 = ((bf16[32,1,20]{2,1,0:T(2,128)(2,1)}), bf16[32,1,20]{2,1,0:T(2,128)(2,1)S(1)}, u32[]{:S(2)}, u32[]{:S(2)}) async-start(bf16[32,1,20]{2,1,0:T(2,128)(2,1)} %reshape.324), calls=%async_computation.3 | async-start | bytes 32768 | tf_op jit(solution)/shard_map/all_to_all | solution.py:223
  35.8 13.2 %all-to-all-start.1 = ((bf16[64,4,1024]{2,0,1:T(8,128)(2,1)}), bf16[64,4,1024]{2,0,1:T(8,128)(2,1)S(1)}, u32[]{:S(2)}, u32[]{:S(2)}) async-start(bf16[64,4,1024]{2,0,1:T(8,128)(2,1)} %copy.255), calls=%async_computation.1 | async-start | bytes 1048576 | tf_op jit(solution)/shard_map/all_to_all | solution.py:300
  39.4 6.3 %collective-permute-start.1 = (bf16[32,20]{0,1:T(8,128)(2,1)S(1)}, bf16[32,20]{0,1:T(8,128)(2,1)S(1)}, u32[]{:S(2)}, u32[]{:S(2)}) collective-permute-start(bf16[32,20]{0,1:T(8,128)(2,1)S(1)} %bitcast.136), channel_id=1, source_target_pairs={{0,32},{32,64},{64,96},{96,0},{1,33},{33,65},{65,97},{97,1},{2,34}... | collective-permute-start | bytes 3848 | tf_op jit(solution)/shard_map/ppermute | solution.py:205
  40.8 6.5 %collective-permute-start = (bf16[32,20]{0,1:T(8,128)(2,1)S(1)}, bf16[32,20]{0,1:T(8,128)(2,1)S(1)}, u32[]{:S(2)}, u32[]{:S(2)}) collective-permute-start(bf16[32,20]{0,1:T(8,128)(2,1)S(1)} %bitcast.137), channel_id=1, source_target_pairs={{0,96},{32,0},{64,32},{96,64},{1,97},{33,1},{65,33},{97,65},{2,98}... | collective-permute-start | bytes 3848 | tf_op jit(solution)/shard_map/ppermute | solution.py:205
  42.1 6.8 %collective-permute-start.2 = (bf16[32,20]{0,1:T(8,128)(2,1)S(1)}, bf16[32,20]{0,1:T(8,128)(2,1)S(1)}, u32[]{:S(2)}, u32[]{:S(2)}) collective-permute-start(bf16[32,20]{0,1:T(8,128)(2,1)S(1)} %bitcast.138), channel_id=1, source_target_pairs={{0,64},{32,96},{64,0},{96,32},{1,65},{33,97},{65,1},{97,33},{2,66}... | collective-permute-start | bytes 3848 | tf_op jit(solution)/shard_map/ppermute | solution.py:205
  49.0 7.8 %all-to-all-start = ((bf16[64,4,128]{2,0,1:T(8,128)(2,1)}), bf16[64,4,128]{2,0,1:T(8,128)(2,1)S(1)}, u32[]{:S(2)}, u32[]{:S(2)}) async-start(bf16[64,4,128]{2,0,1:T(8,128)(2,1)} %copy.254), calls=%async_computation | async-start | bytes 131072 | tf_op jit(solution)/shard_map/all_to_all | solution.py:301
  56.8 7.7 %all-to-all-start.2 = ((bf16[64,4,128]{2,0,1:T(8,128)(2,1)}), bf16[64,4,128]{2,0,1:T(8,128)(2,1)S(1)}, u32[]{:S(2)}, u32[]{:S(2)}) async-start(bf16[64,4,128]{2,0,1:T(8,128)(2,1)} %copy.257), calls=%async_computation.2 | async-start | bytes 131072 | tf_op jit(solution)/shard_map/all_to_all | solution.py:302
  71.6 10.0 %collective-permute-start.8 = (bf16[64,2048]{1,0:T(8,128)(2,1)S(1)}, bf16[64,2048]{1,0:T(8,128)(2,1)S(1)}, u32[]{:S(2)}, u32[]{:S(2)}) collective-permute-start(bf16[64,2048]{1,0:T(8,128)(2,1)S(1)} %get-tuple-element.30), channel_id=1, source_target_pairs={{0,96},{32,0},{64,32},{96,64},{1,97},{33,1},{65,33},{97,65},{2,98}... | collective-permute-start | bytes 786440 | tf_op jit(solution)/shard_map/ppermute | solution.py:205
  74.3 8.1 %collective-permute-start.7 = (bf16[64,2048]{1,0:T(8,128)(2,1)S(1)}, bf16[64,2048]{1,0:T(8,128)(2,1)}, u32[]{:S(2)}, u32[]{:S(2)}) collective-permute-start(bf16[64,2048]{1,0:T(8,128)(2,1)S(1)} %get-tuple-element.29), channel_id=1, source_target_pairs={{0,64},{32,96},{64,0},{96,32},{1,65},{33,97},{65,1},{97,33},{2,66}... | collective-permute-start | bytes 786440 | tf_op jit(solution)/shard_map/ppermute | solution.py:205
  74.7 16.7 %collective-permute-start.6 = (bf16[64,2048]{1,0:T(8,128)(2,1)S(1)}, bf16[64,2048]{1,0:T(8,128)(2,1)}, u32[]{:S(2)}, u32[]{:S(2)}) collective-permute-start(bf16[64,2048]{1,0:T(8,128)(2,1)S(1)} %get-tuple-element.28), channel_id=1, source_target_pairs={{0,32},{32,64},{64,96},{96,0},{1,33},{33,65},{65,97},{97,1},{2,34}... | collective-permute-start | bytes 786440 | tf_op jit(solution)/shard_map/ppermute | solution.py:205
  77.2 15.6 %collective-permute-start.11 = (bf16[64,2048]{1,0:T(8,128)(2,1)S(1)}, bf16[64,2048]{1,0:T(8,128)(2,1)S(1)}, u32[]{:S(2)}, u32[]{:S(2)}) collective-permute-start(bf16[64,2048]{1,0:T(8,128)(2,1)S(1)} %get-tuple-element.34), channel_id=1, source_target_pairs={{0,96},{32,0},{64,32},{96,64},{1,97},{33,1},{65,33},{97,65},{2,98}... | collective-permute-start | bytes 786440 | tf_op jit(solution)/shard_map/ppermute | solution.py:205
  79.5 14.1 %collective-permute-start.10 = (bf16[64,2048]{1,0:T(8,128)(2,1)S(1)}, bf16[64,2048]{1,0:T(8,128)(2,1)S(1)}, u32[]{:S(2)}, u32[]{:S(2)}) collective-permute-start(bf16[64,2048]{1,0:T(8,128)(2,1)S(1)} %get-tuple-element.33), channel_id=1, source_target_pairs={{0,64},{32,96},{64,0},{96,32},{1,65},{33,97},{65,1},{97,33},{2,66}... | collective-permute-start | bytes 786440 | tf_op jit(solution)/shard_map/ppermute | solution.py:205
  81.6 19.3 %collective-permute-start.9 = (bf16[64,2048]{1,0:T(8,128)(2,1)S(1)}, bf16[64,2048]{1,0:T(8,128)(2,1)}, u32[]{:S(2)}, u32[]{:S(2)}) collective-permute-start(bf16[64,2048]{1,0:T(8,128)(2,1)S(1)} %get-tuple-element.32), channel_id=1, source_target_pairs={{0,32},{32,64},{64,96},{96,0},{1,33},{33,65},{65,97},{97,1},{2,34}... | collective-permute-start | bytes 786440 | tf_op jit(solution)/shard_map/ppermute | solution.py:205
  105.1 28.0 %all-to-all-start.4 = ((bf16[32,24,1024]{2,1,0:T(8,128)(2,1)}), bf16[32,24,1024]{2,1,0:T(8,128)(2,1)S(1)}, u32[]{:S(2)}, u32[]{:S(2)}) async-start(bf16[32,24,1024]{2,1,0:T(8,128)(2,1)} %bitcast.118), calls=%async_computation.4 | async-start | bytes 3145728 | tf_op jit(solution)/shard_map/all_to_all | solution.py:223
  112.0 22.2 %collective-permute-start.12 = (bf16[64,4096]{1,0:T(8,128)(2,1)}, bf16[64,4096]{1,0:T(8,128)(2,1)}, u32[]{:S(2)}, u32[]{:S(2)}) collective-permute-start(bf16[64,4096]{1,0:T(8,128)(2,1)} %multiply_convert_fusion), channel_id=1, source_target_pairs={{0,96},{32,0},{64,32},{96,64},{1,97},{33,1},{65,33},{97,65},{2,98}... | collective-permute-start | bytes 1572872 | tf_op jit(solution)/shard_map/ppermute | solution.py:205
  112.3 21.9 %collective-permute-start.13 = (bf16[64,4096]{1,0:T(8,128)(2,1)}, bf16[64,4096]{1,0:T(8,128)(2,1)}, u32[]{:S(2)}, u32[]{:S(2)}) collective-permute-start(bf16[64,4096]{1,0:T(8,128)(2,1)} %multiply_convert_fusion), channel_id=1, source_target_pairs={{0,64},{32,96},{64,0},{96,32},{1,65},{33,97},{65,1},{97,33},{2,66}... | collective-permute-start | bytes 1572872 | tf_op jit(solution)/shard_map/ppermute | solution.py:205
  112.9 26.3 %collective-permute-start.14 = (bf16[64,4096]{1,0:T(8,128)(2,1)}, bf16[64,4096]{1,0:T(8,128)(2,1)}, u32[]{:S(2)}, u32[]{:S(2)}) collective-permute-start(bf16[64,4096]{1,0:T(8,128)(2,1)} %multiply_convert_fusion), channel_id=1, source_target_pairs={{0,32},{32,64},{64,96},{96,0},{1,33},{33,65},{65,97},{97,1},{2,34}... | collective-permute-start | bytes 1572872 | tf_op jit(solution)/shard_map/ppermute | solution.py:205
  139.2 36.8 %collective-permute-start.15 = (bf16[192,4096]{1,0:T(8,128)(2,1)S(1)}, bf16[192,4096]{1,0:T(8,128)(2,1)}, u32[]{:S(2)}, u32[]{:S(2)}) collective-permute-start(bf16[192,4096]{1,0:T(8,128)(2,1)S(1)} %reshape.304.refs_0_), channel_id=1, source_target_pairs={{0,32},{32,64},{64,96},{96,0},{1,33},{33,65},{65,97},{97,1},{2,34}... | collective-permute-start | bytes 4718600 | tf_op jit(solution)/shard_map/ppermute | solution.py:205
  139.2 38.1 %collective-permute-start.17 = (bf16[192,4096]{1,0:T(8,128)(2,1)S(1)}, bf16[192,4096]{1,0:T(8,128)(2,1)S(1)}, u32[]{:S(2)}, u32[]{:S(2)}) collective-permute-start(bf16[192,4096]{1,0:T(8,128)(2,1)S(1)} %reshape.304.refs_0_), channel_id=1, source_target_pairs={{0,96},{32,0},{64,32},{96,64},{1,97},{33,1},{65,33},{97,65},{2,98}... | collective-permute-start | bytes 4718600 | tf_op jit(solution)/shard_map/ppermute | solution.py:205
  147.9 58.4 %all-to-all-start.5 = ((bf16[32,16,4096]{2,1,0:T(8,128)(2,1)}), bf16[32,16,4096]{2,1,0:T(8,128)(2,1)}, u32[]{:S(2)}, u32[]{:S(2)}) async-start(bf16[32,16,4096]{2,1,0:T(8,128)(2,1)} %bitcast.119), calls=%async_computation.5 | async-start | bytes 8388608 | tf_op jit(solution)/shard_map/all_to_all | solution.py:223
  156.1 116.6 %reduce-scatter.2.cloned.1.call-start = ((), (), s32[]{:S(2)}) async-start(), calls=%async_computation.10 | async-start | bytes 7864320 | tf_op jit(solution)/shard_map/reduce_scatter | solution.py:367
  177.2 19.7 %collective-permute-start.16 = (bf16[96,4096]{1,0:T(8,128)(2,1)S(1)}, bf16[96,4096]{1,0:T(8,128)(2,1)S(1)}, u32[]{:S(2)}, u32[]{:S(2)}) collective-permute-start(bf16[96,4096]{1,0:T(8,128)(2,1)S(1)} %slice.94), channel_id=1, source_target_pairs={{0,32},{32,64},{64,96},{96,0},{1,33},{33,65},{65,97},{97,1},{2,34}... | collective-permute-start | bytes 2359304 | tf_op jit(solution)/shard_map/ppermute | solution.py:205
  177.3 19.6 %collective-permute-start.18 = (bf16[96,4096]{1,0:T(8,128)(2,1)S(1)}, bf16[96,4096]{1,0:T(8,128)(2,1)S(1)}, u32[]{:S(2)}, u32[]{:S(2)}) collective-permute-start(bf16[96,4096]{1,0:T(8,128)(2,1)S(1)} %slice.95), channel_id=1, source_target_pairs={{0,96},{32,0},{64,32},{96,64},{1,97},{33,1},{65,33},{97,65},{2,98}... | collective-permute-start | bytes 2359304 | tf_op jit(solution)/shard_map/ppermute | solution.py:205
  222.6 58.8 %all-to-all-start.7 = ((bf16[32,16,4096]{2,1,0:T(8,128)(2,1)}), bf16[32,16,4096]{2,1,0:T(8,128)(2,1)}, u32[]{:S(2)}, u32[]{:S(2)}) async-start(bf16[32,16,4096]{2,1,0:T(8,128)(2,1)} %bitcast.120), calls=%async_computation.8 | async-start | bytes 8388608 | tf_op jit(solution)/shard_map/all_to_all | solution.py:223
  281.3 30.1 %all-to-all-start.6 = ((bf16[32,24,1024]{2,1,0:T(8,128)(2,1)}), bf16[32,24,1024]{2,1,0:T(8,128)(2,1)}, u32[]{:S(2)}, u32[]{:S(2)}) async-start(bf16[32,24,1024]{2,1,0:T(8,128)(2,1)} %reshape.307), calls=%async_computation.7 | async-start | bytes 3145728 | tf_op jit(solution)/shard_map/all_to_all | solution.py:223
  293.8 24.9 %collective-permute-start.21 = (bf16[64,4096]{1,0:T(8,128)(2,1)}, bf16[64,4096]{1,0:T(8,128)(2,1)S(1)}, u32[]{:S(2)}, u32[]{:S(2)}) collective-permute-start(bf16[64,4096]{1,0:T(8,128)(2,1)} %get-tuple-element.48), channel_id=1, source_target_pairs={{0,96},{32,0},{64,32},{96,64},{1,97},{33,1},{65,33},{97,65},{2,98}... | collective-permute-start | bytes 1572872 | tf_op jit(solution)/shard_map/ppermute | solution.py:205
  296.5 22.3 %collective-permute-start.20 = (bf16[64,4096]{1,0:T(8,128)(2,1)}, bf16[64,4096]{1,0:T(8,128)(2,1)}, u32[]{:S(2)}, u32[]{:S(2)}) collective-permute-start(bf16[64,4096]{1,0:T(8,128)(2,1)} %get-tuple-element.49), channel_id=1, source_target_pairs={{0,64},{32,96},{64,0},{96,32},{1,65},{33,97},{65,1},{97,33},{2,66}... | collective-permute-start | bytes 1572872 | tf_op jit(solution)/shard_map/ppermute | solution.py:205
  296.5 26.3 %collective-permute-start.19 = (bf16[64,4096]{1,0:T(8,128)(2,1)}, bf16[64,4096]{1,0:T(8,128)(2,1)}, u32[]{:S(2)}, u32[]{:S(2)}) collective-permute-start(bf16[64,4096]{1,0:T(8,128)(2,1)} %get-tuple-element.47), channel_id=1, source_target_pairs={{0,32},{32,64},{64,96},{96,0},{1,33},{33,65},{65,97},{97,1},{2,34}... | collective-permute-start | bytes 1572872 | tf_op jit(solution)/shard_map/ppermute | solution.py:205
  (18 other events, 305.9 us)
Sparse Core Ops, SparseCore 0:
  9.6 56.6 all-gather.1
  206.5 66.1 reduce-scatter.1

commit v4 on v3

--- a/solution.py
+++ b/solution.py
@@ -368,12 +368,13 @@
         parts.reshape(-1, model_width), "seq", scatter_dimension=0, tiled=True
     )
     shared_back = across(shared_sums.reshape(columns, SHARED_SLOTS * ROW_PIECES, -1))
-    pack_sums = jnp.einsum(
-        "rq,qm->rm",
-        direct_mask,
-        direct_back.reshape(direct_count, model_width),
-        preferred_element_type=jnp.float32,
-    ).astype(jnp.bfloat16)
+    back_rows = direct_back.reshape(direct_count, model_width)
+    pack_sums = [
+        jnp.einsum("rq,qm->rm", mask, back_rows, preferred_element_type=jnp.float32).astype(
+            jnp.bfloat16
+        )
+        for mask in by_owner(direct_mask)
+    ]
     shared_total = jnp.einsum(
         "qa,qc->ac",
         shared_mask,
@@ -383,7 +384,7 @@
     total = hidden + shared_total.reshape(ROW_PIECES, token_count, -1).swapaxes(0, 1).reshape(
         token_count, model_width
     )
-    for part in back_around(by_owner(pack_sums)):
+    for part in back_around(pack_sums):
         total = total + part.astype(jnp.float32)
     return total.astype(jnp.bfloat16)[None]
 

time: 333 us -> 342 us (1.027)
  matrix products: 14.7 us -> 25 us
    dot_general x1 -> x4, matrix products: 3.46 us -> 16.2 us  [local(): jnp.einsum('rq,qm->rm', mask, back_rows, preferred_element_type=jnp.float32)]
    ppermute x22, waiting for transfers between devices: 57.9 us -> 66.6 us  [ring(): lax.ppermute(rows, 'seq', [(i, (i + step) % count) for i in range(count)])]
    all_to_all x5, waiting for transfers between devices: 39.4 us -> 32.2 us  [across(): lax.all_to_all(blocks, 'exp', split_axis=0, concat_axis=0, tiled=True)]
  transfers between devices with their start and end apart: 32 -> 32, of which waited for: 21 -> 19; matrix products, arithmetic and copies ran while one was open for 11% -> 12% of each run, Pallas kernels for 13% -> 13%
where the time goes in v4:
time: 342 us; the launch traced here: 341 us
  waiting for transfers between devices  148 us (43%)
  starting transfers between devices  77 us (23%)
  Pallas kernels  44.5 us (13%)
  matrix products  25 us (7%)
  local copies, waits for them, and re-layouts  24.7 us (7%)
  between operations  14.2 us (4%)
  other arithmetic  6.87 us (2%)
    ppermute x22, waiting for transfers between devices, ring(): lax.ppermute(rows, 'seq', [(i, (i + step) % count) for i in range(count)])  66.6 us
    reduce_scatter x1, waiting for transfers between devices, local(): lax.psum_scatter(parts.reshape(-1, model_width), 'seq', scatter_dimension...  41.6 us
    pallas_call x3, Pallas kernels, expert(): pl.pallas_call(functools.partial(expert_kernel, sizes, places, aliased),...  40.8 us
    all_to_all x5, starting transfers between devices, across(): lax.all_to_all(blocks, 'exp', split_axis=0, concat_axis=0, tiled=True)  38.1 us
    all_to_all x5, waiting for transfers between devices, across(): lax.all_to_all(blocks, 'exp', split_axis=0, concat_axis=0, tiled=True)  32.2 us
    ppermute x22, starting transfers between devices, ring(): lax.ppermute(rows, 'seq', [(i, (i + step) % count) for i in range(count)])  28.8 us
    dot_general x4, matrix products, local(): jnp.einsum('rq,qm->rm', mask, back_rows, preferred_element_type=jnp.float32)  16.2 us
  transfers between devices with their start and end apart: 32, of which 19 were waited for; matrix products, arithmetic and copies ran while one was open for 12% of the time, Pallas kernels for 13%

profile of v4, /device:TPU:1, one launch (start us, length us, event | category | flops | bytes accessed | tf_op | source)
XLA Modules:
  0.0 340.5 jit_solution(13037991407532190838)
XLA Ops:
  9.8 3.3 collective-permute-start.4
  17.3 8.6 %all-to-all-start.3 = ((bf16[32,1,20]{2,1,0:T(2,128)(2,1)}), bf16[32,1,20]{2,1,0:T(2,128)(2,1)S(1)}, u32[]{:S(2)}, u32[]{:S(2)}) async-start(bf16[32,1,20]{2,1,0:T(2,128)(2,1)} %reshape.324), calls=%async_computation.3 | async-start | bytes 32768 | tf_op jit(solution)/shard_map/all_to_all | solution.py:223
  35.2 3.5 %all-to-all-start.1 = ((bf16[64,4,1024]{2,0,1:T(8,128)(2,1)}), bf16[64,4,1024]{2,0,1:T(8,128)(2,1)S(1)}, u32[]{:S(2)}, u32[]{:S(2)}) async-start(bf16[64,4,1024]{2,0,1:T(8,128)(2,1)} %copy.255), calls=%async_computation.1 | async-start | bytes 1048576 | tf_op jit(solution)/shard_map/all_to_all | solution.py:300
  48.4 3.3 all-to-all-start
  56.2 3.3 all-to-all-start.2
  60.2 3.7 %all-to-all-done.2 = bf16[64,4,128]{2,0,1:T(8,128)(2,1)S(1)} async-done(((bf16[64,4,128]{2,0,1:T(8,128)(2,1)}), bf16[64,4,128]{2,0,1:T(8,128)(2,1)S(1)}, u32[]{:S(2)}, u32[]{:S(2)}) %all-to-all-start.2) | async-done | bytes 65568 | tf_op jit(solution)/shard_map/all_to_all | solution.py:302
  66.3 3.4 copy-done
  83.2 7.6 %collective-permute-done.6 = bf16[64,2048]{1,0:T(8,128)(2,1)} collective-permute-done((bf16[64,2048]{1,0:T(8,128)(2,1)S(1)}, bf16[64,2048]{1,0:T(8,128)(2,1)}, u32[]{:S(2)}, u32[]{:S(2)}) %collective-permute-start.6) | collective-permute-done | bytes 262176 | tf_op jit(solution)/shard_map/ppermute | solution.py:205
  90.8 5.5 %collective-permute-done.11 = bf16[64,2048]{1,0:T(8,128)(2,1)S(1)} collective-permute-done((bf16[64,2048]{1,0:T(8,128)(2,1)S(1)}, bf16[64,2048]{1,0:T(8,128)(2,1)S(1)}, u32[]{:S(2)}, u32[]{:S(2)}) %collective-permute-start.11) | collective-permute-done | bytes 262176 | tf_op jit(solution)/shard_map/ppermute | solution.py:205
  96.3 4.6 %collective-permute-done.9 = bf16[64,2048]{1,0:T(8,128)(2,1)} collective-permute-done((bf16[64,2048]{1,0:T(8,128)(2,1)S(1)}, bf16[64,2048]{1,0:T(8,128)(2,1)}, u32[]{:S(2)}, u32[]{:S(2)}) %collective-permute-start.9) | collective-permute-done | bytes 262176 | tf_op jit(solution)/shard_map/ppermute | solution.py:205
  105.1 5.8 %all-to-all-start.4 = ((bf16[32,24,1024]{2,1,0:T(8,128)(2,1)}), bf16[32,24,1024]{2,1,0:T(8,128)(2,1)S(1)}, u32[]{:S(2)}, u32[]{:S(2)}) async-start(bf16[32,24,1024]{2,1,0:T(8,128)(2,1)} %bitcast.121), calls=%async_computation.4 | async-start | bytes 3145728 | tf_op jit(solution)/shard_map/all_to_all | solution.py:223
  113.4 19.7 %all-to-all-done.4 = bf16[32,24,1024]{2,1,0:T(8,128)(2,1)S(1)} async-done(((bf16[32,24,1024]{2,1,0:T(8,128)(2,1)}), bf16[32,24,1024]{2,1,0:T(8,128)(2,1)S(1)}, u32[]{:S(2)}, u32[]{:S(2)}) %all-to-all-start.4) | async-done | bytes 1572896 | tf_op jit(solution)/shard_map/all_to_all | solution.py:223
  134.2 5.0 %collective-permute-done.14 = bf16[64,4096]{1,0:T(8,128)(2,1)} collective-permute-done((bf16[64,4096]{1,0:T(8,128)(2,1)}, bf16[64,4096]{1,0:T(8,128)(2,1)}, u32[]{:S(2)}, u32[]{:S(2)}) %collective-permute-start.14) | collective-permute-done | bytes 524320 | tf_op jit(solution)/shard_map/ppermute | solution.py:205
  143.0 4.9 %convolution_convert_fusion = bf16[512,4096]{1,0:T(8,128)(2,1)} fusion(bf16[256,512]{0,1:T(8,128)(2,1)} %add_convert_fusion.1, bf16[64,4096]{1,0:T(8,128)(2,1)} %collective-permute-done.14, bf16[64,4096]{1,0:T(8,128)(2,1)} %collective-permute-done.13, bf16[64,4096]{1,0:T(8,128)(2,1)} %collective-permute-done.12, bf16[64,4096]{1,0:T(8,128)(2,1)} %multiply_convert_fusion), kind=kOutput, calls=%fused_computation | convolution fusion | flops 1084227584 | bytes 6553600 | tf_op jit(solution)/shard_map/rq,rm->qm/dot_general | solution.py:344
  148.0 8.1 %all-to-all-start.5 = ((bf16[32,16,4096]{2,1,0:T(8,128)(2,1)}), bf16[32,16,4096]{2,1,0:T(8,128)(2,1)}, u32[]{:S(2)}, u32[]{:S(2)}) async-start(bf16[32,16,4096]{2,1,0:T(8,128)(2,1)} %bitcast.122), calls=%async_computation.5 | async-start | bytes 8388608 | tf_op jit(solution)/shard_map/all_to_all | solution.py:223
  156.1 19.9 %collective-permute-done.15.refs_2_ = bf16[192,4096]{1,0:T(8,128)(2,1)} collective-permute-done((bf16[192,4096]{1,0:T(8,128)(2,1)S(1)}, bf16[192,4096]{1,0:T(8,128)(2,1)}, u32[]{:S(2)}, u32[]{:S(2)}) %collective-permute-start.15) | collective-permute-done | bytes 1572896 | tf_op jit(solution)/shard_map/ppermute | solution.py:205
  177.3 2.9 collective-permute-start.18
  180.3 16.6 %expert.3.refs_6_ = bf16[4,192,4096]{2,1,0:T(8,128)(2,1)} custom-call(bf16[192,4096]{1,0:T(8,128)(2,1)S(1)} %reshape.304.refs_0_, bf16[192,4096]{1,0:T(8,128)(2,1)S(1)} %collective-permute-done.17.refs_1_, bf16[192,4096]{1,0:T(8,128)(2,1)} %collective-permute-done.15.refs_2_, f32[576,1]{1,0:T(8,128)S(1)} %copy.287.refs_3_, bf16[4096,768]{1,0:T(8,128)(2,1)} %bitcast.147, ...), custom_call_target="tpu_custom_call" | custom-call | flops 108716359680 | bytes 28311552 | tf_op jit(solution)/shard_map/expert/pallas_call | solution.py:137
  196.9 8.9 %expert.4 = bf16[4,192,4096]{2,1,0:T(8,128)(2,1)} custom-call(bf16[96,4096]{1,0:T(8,128)(2,1)S(1)} %collective-permute-done.16.refs_0_, bf16[96,4096]{1,0:T(8,128)(2,1)S(1)} %collective-permute-done.18.refs_1_, f32[192,1]{1,0:T(8,128)S(1)} %copy.288.refs_2_, bf16[4096,768]{1,0:T(8,128)(2,1)} %bitcast.148, ...), custom_call_target="tpu_custom_call", output_to_operand_aliasing={{}: (6, {})} | custom-call | flops 36238786560 | bytes 22020096 | tf_op jit(solution)/shard_map/expert/pallas_call | solution.py:137
  207.3 15.3 %expert.5 = bf16[1,512,4096]{2,1,0:T(8,128)(2,1)} custom-call(bf16[512,4096]{1,0:T(8,128)(2,1)} %bitcast.51.refs_0_, f32[512,1]{1,0:T(8,128)S(1)} %copy-done.1, bf16[4096,768]{1,0:T(8,128)(2,1)} %bitcast.149, bf16[4096,768]{1,0:T(8,128)(2,1)} %bitcast.152, bf16[768,4096]{1,0:T(8,128)(2,1)} %bitcast.155), custom_call_target="tpu_custom_call" | custom-call | flops 96636764160 | bytes 27262976 | tf_op jit(solution)/shard_map/expert/pallas_call | solution.py:137
  222.6 8.4 %all-to-all-start.7 = ((bf16[32,16,4096]{2,1,0:T(8,128)(2,1)}), bf16[32,16,4096]{2,1,0:T(8,128)(2,1)}, u32[]{:S(2)}, u32[]{:S(2)}) async-start(bf16[32,16,4096]{2,1,0:T(8,128)(2,1)} %bitcast.123), calls=%async_computation.8 | async-start | bytes 8388608 | tf_op jit(solution)/shard_map/all_to_all | solution.py:223
  231.1 41.6 %reduce-scatter.2.cloned.1.call-done = bf16[192,4096]{1,0:T(8,128)(2,1)} async-done(((bf16[768,4096]{1,0:T(8,128)(2,1)}), bf16[192,4096]{1,0:T(8,128)(2,1)}) %reduce-scatter.2.cloned.1.call-update) | async-done | bytes 1572880 | tf_op jit(solution)/shard_map/reduce_scatter | solution.py:367
  272.7 3.7 %reshape.307 = bf16[32,24,1024]{2,1,0:T(8,128)(2,1)} reshape(bf16[192,4096]{1,0:T(8,128)(2,1)} %reduce-scatter.2.cloned.1.call-done) | data formatting | bytes 3145728 | tf_op jit(solution)/shard_map/reshape | solution.py:370
  276.4 4.9 %all-to-all-done.7 = bf16[32,16,4096]{2,1,0:T(8,128)(2,1)} async-done(((bf16[32,16,4096]{2,1,0:T(8,128)(2,1)}), bf16[32,16,4096]{2,1,0:T(8,128)(2,1)}, u32[]{:S(2)}, u32[]{:S(2)}) %all-to-all-start.7) | async-done | bytes 4194336 | tf_op jit(solution)/shard_map/all_to_all | solution.py:223
  281.3 7.1 %all-to-all-start.6 = ((bf16[32,24,1024]{2,1,0:T(8,128)(2,1)}), bf16[32,24,1024]{2,1,0:T(8,128)(2,1)S(1)}, u32[]{:S(2)}, u32[]{:S(2)}) async-start(bf16[32,24,1024]{2,1,0:T(8,128)(2,1)} %reshape.307), calls=%async_computation.7 | async-start | bytes 3145728 | tf_op jit(solution)/shard_map/all_to_all | solution.py:223
  288.5 3.9 %convolution_convert_fusion.1 = bf16[64,4096]{1,0:T(8,128)(2,1)} fusion(bf16[512,4096]{1,0:T(8,128)(2,1)} %bitcast.53, bf16[256,512]{0,1:T(8,128)(2,1)S(1)} %copy-done.8), kind=kOutput, calls=%fused_computation.1 | convolution fusion | flops 268697600 | bytes 4849664 | tf_op jit(solution)/shard_map/rq,qm->rm/dot_general | solution.py:373
  292.4 3.9 %convolution_convert_fusion.2 = bf16[64,4096]{1,0:T(8,128)(2,1)} fusion(bf16[512,4096]{1,0:T(8,128)(2,1)} %bitcast.53, bf16[256,512]{0,1:T(8,128)(2,1)S(1)} %copy-done.8), kind=kOutput, calls=%fused_computation.2 | convolution fusion | flops 268697600 | bytes 4849664 | tf_op jit(solution)/shard_map/rq,qm->rm/dot_general | solution.py:373
  296.3 4.0 %convolution_convert_fusion.3 = bf16[64,4096]{1,0:T(8,128)(2,1)} fusion(bf16[512,4096]{1,0:T(8,128)(2,1)} %bitcast.53, bf16[256,512]{0,1:T(8,128)(2,1)S(1)} %copy-done.8), kind=kOutput, calls=%fused_computation.3 | convolution fusion | flops 268697600 | bytes 4849664 | tf_op jit(solution)/shard_map/rq,qm->rm/dot_general | solution.py:373
  303.7 7.1 %all-to-all-done.6 = bf16[32,24,1024]{2,1,0:T(8,128)(2,1)S(1)} async-done(((bf16[32,24,1024]{2,1,0:T(8,128)(2,1)}), bf16[32,24,1024]{2,1,0:T(8,128)(2,1)S(1)}, u32[]{:S(2)}, u32[]{:S(2)}) %all-to-all-start.6) | async-done | bytes 1572896 | tf_op jit(solution)/shard_map/all_to_all | solution.py:223
  311.4 13.9 %collective-permute-done.21 = bf16[64,4096]{1,0:T(8,128)(2,1)S(1)} collective-permute-done((bf16[64,4096]{1,0:T(8,128)(2,1)}, bf16[64,4096]{1,0:T(8,128)(2,1)S(1)}, u32[]{:S(2)}, u32[]{:S(2)}) %collective-permute-start.21) | collective-permute-done | bytes 524320 | tf_op jit(solution)/shard_map/ppermute | solution.py:205
  325.3 3.9 %collective-permute-done.19 = bf16[64,4096]{1,0:T(8,128)(2,1)} collective-permute-done((bf16[64,4096]{1,0:T(8,128)(2,1)}, bf16[64,4096]{1,0:T(8,128)(2,1)}, u32[]{:S(2)}, u32[]{:S(2)}) %collective-permute-start.19) | collective-permute-done | bytes 524320 | tf_op jit(solution)/shard_map/ppermute | solution.py:205
  329.3 4.4 %fusion.12 = bf16[1,64,4096]{2,1,0:T(8,128)(2,1)} fusion(bf16[64,4096]{1,0:T(8,128)(2,1)S(1)} %collective-permute-done.21, bf16[64,4096]{1,0:T(8,128)(2,1)} %collective-permute-done.20, bf16[64,4096]{1,0:T(8,128)(2,1)} %collective-permute-done.19, f32[64,4096]{1,0:T(8,128)S(1)} %bitcast.124, f32[64,2048]{1,0:T(8,128)S(1)} %copy-done.5, ...), kind=kOutput, calls=%fused_computation.32 | convolution fusion | flops 271581184 | bytes 8519680 | tf_op jit(solution)/shard_map/rq,qm->rm/dot_general | solution.py:373
  (198 shorter events, 65.4 us)
Async XLA Ops:
  6.5 59.8 %all-gather.2.cloned.1.call-start = ((), (), s32[]{:S(2)}) async-start(), calls=%async_computation.9 | async-start | bytes 8650752 | tf_op jit(solution)/shard_map/all_gather | solution.py:317
  7.3 25.3 %collective-permute-start.5 = (s32[64,4]{0,1:T(4,128)}, s32[64,4]{0,1:T(4,128)S(1)}, u32[]{:S(2)}, u32[]{:S(2)}) collective-permute-start(s32[64,4]{0,1:T(4,128)} %bitcast.143), channel_id=1, source_target_pairs={{0,32},{32,64},{64,96},{96,0},{1,33},{33,65},{65,97},{97,1},{2,34}... | collective-permute-start | bytes 3080 | tf_op jit(solution)/shard_map/ppermute | solution.py:205
  9.8 22.8 %collective-permute-start.4 = (s32[64,4]{0,1:T(4,128)}, s32[64,4]{0,1:T(4,128)S(1)}, u32[]{:S(2)}, u32[]{:S(2)}) collective-permute-start(s32[64,4]{0,1:T(4,128)} %bitcast.144), channel_id=1, source_target_pairs={{0,64},{32,96},{64,0},{96,32},{1,65},{33,97},{65,1},{97,33},{2,66}... | collective-permute-start | bytes 3080 | tf_op jit(solution)/shard_map/ppermute | solution.py:205
  13.1 20.0 %collective-permute-start.3 = (s32[64,4]{0,1:T(4,128)}, s32[64,4]{0,1:T(4,128)S(1)}, u32[]{:S(2)}, u32[]{:S(2)}) collective-permute-start(s32[64,4]{0,1:T(4,128)} %bitcast.145), channel_id=1, source_target_pairs={{0,96},{32,0},{64,32},{96,64},{1,97},{33,1},{65,33},{97,65},{2,98}... | collective-permute-start | bytes 3080 | tf_op jit(solution)/shard_map/ppermute | solution.py:205
  17.3 17.9 %all-to-all-start.3 = ((bf16[32,1,20]{2,1,0:T(2,128)(2,1)}), bf16[32,1,20]{2,1,0:T(2,128)(2,1)S(1)}, u32[]{:S(2)}, u32[]{:S(2)}) async-start(bf16[32,1,20]{2,1,0:T(2,128)(2,1)} %reshape.324), calls=%async_computation.3 | async-start | bytes 32768 | tf_op jit(solution)/shard_map/all_to_all | solution.py:223
  35.2 13.2 %all-to-all-start.1 = ((bf16[64,4,1024]{2,0,1:T(8,128)(2,1)}), bf16[64,4,1024]{2,0,1:T(8,128)(2,1)S(1)}, u32[]{:S(2)}, u32[]{:S(2)}) async-start(bf16[64,4,1024]{2,0,1:T(8,128)(2,1)} %copy.255), calls=%async_computation.1 | async-start | bytes 1048576 | tf_op jit(solution)/shard_map/all_to_all | solution.py:300
  38.8 6.3 %collective-permute-start.1 = (bf16[32,20]{0,1:T(8,128)(2,1)S(1)}, bf16[32,20]{0,1:T(8,128)(2,1)S(1)}, u32[]{:S(2)}, u32[]{:S(2)}) collective-permute-start(bf16[32,20]{0,1:T(8,128)(2,1)S(1)} %bitcast.139), channel_id=1, source_target_pairs={{0,32},{32,64},{64,96},{96,0},{1,33},{33,65},{65,97},{97,1},{2,34}... | collective-permute-start | bytes 3848 | tf_op jit(solution)/shard_map/ppermute | solution.py:205
  40.2 6.4 %collective-permute-start = (bf16[32,20]{0,1:T(8,128)(2,1)S(1)}, bf16[32,20]{0,1:T(8,128)(2,1)S(1)}, u32[]{:S(2)}, u32[]{:S(2)}) collective-permute-start(bf16[32,20]{0,1:T(8,128)(2,1)S(1)} %bitcast.140), channel_id=1, source_target_pairs={{0,96},{32,0},{64,32},{96,64},{1,97},{33,1},{65,33},{97,65},{2,98}... | collective-permute-start | bytes 3848 | tf_op jit(solution)/shard_map/ppermute | solution.py:205
  41.5 6.8 %collective-permute-start.2 = (bf16[32,20]{0,1:T(8,128)(2,1)S(1)}, bf16[32,20]{0,1:T(8,128)(2,1)S(1)}, u32[]{:S(2)}, u32[]{:S(2)}) collective-permute-start(bf16[32,20]{0,1:T(8,128)(2,1)S(1)} %bitcast.141), channel_id=1, source_target_pairs={{0,64},{32,96},{64,0},{96,32},{1,65},{33,97},{65,1},{97,33},{2,66}... | collective-permute-start | bytes 3848 | tf_op jit(solution)/shard_map/ppermute | solution.py:205
  48.4 7.8 %all-to-all-start = ((bf16[64,4,128]{2,0,1:T(8,128)(2,1)}), bf16[64,4,128]{2,0,1:T(8,128)(2,1)S(1)}, u32[]{:S(2)}, u32[]{:S(2)}) async-start(bf16[64,4,128]{2,0,1:T(8,128)(2,1)} %copy.254), calls=%async_computation | async-start | bytes 131072 | tf_op jit(solution)/shard_map/all_to_all | solution.py:301
  56.2 7.8 %all-to-all-start.2 = ((bf16[64,4,128]{2,0,1:T(8,128)(2,1)}), bf16[64,4,128]{2,0,1:T(8,128)(2,1)S(1)}, u32[]{:S(2)}, u32[]{:S(2)}) async-start(bf16[64,4,128]{2,0,1:T(8,128)(2,1)} %copy.257), calls=%async_computation.2 | async-start | bytes 131072 | tf_op jit(solution)/shard_map/all_to_all | solution.py:302
  71.6 11.0 %collective-permute-start.8 = (bf16[64,2048]{1,0:T(8,128)(2,1)S(1)}, bf16[64,2048]{1,0:T(8,128)(2,1)S(1)}, u32[]{:S(2)}, u32[]{:S(2)}) collective-permute-start(bf16[64,2048]{1,0:T(8,128)(2,1)S(1)} %get-tuple-element.30), channel_id=1, source_target_pairs={{0,96},{32,0},{64,32},{96,64},{1,97},{33,1},{65,33},{97,65},{2,98}... | collective-permute-start | bytes 786440 | tf_op jit(solution)/shard_map/ppermute | solution.py:205
  74.3 8.9 %collective-permute-start.7 = (bf16[64,2048]{1,0:T(8,128)(2,1)S(1)}, bf16[64,2048]{1,0:T(8,128)(2,1)}, u32[]{:S(2)}, u32[]{:S(2)}) collective-permute-start(bf16[64,2048]{1,0:T(8,128)(2,1)S(1)} %get-tuple-element.29), channel_id=1, source_target_pairs={{0,64},{32,96},{64,0},{96,32},{1,65},{33,97},{65,1},{97,33},{2,66}... | collective-permute-start | bytes 786440 | tf_op jit(solution)/shard_map/ppermute | solution.py:205
  74.7 16.1 %collective-permute-start.6 = (bf16[64,2048]{1,0:T(8,128)(2,1)S(1)}, bf16[64,2048]{1,0:T(8,128)(2,1)}, u32[]{:S(2)}, u32[]{:S(2)}) collective-permute-start(bf16[64,2048]{1,0:T(8,128)(2,1)S(1)} %get-tuple-element.28), channel_id=1, source_target_pairs={{0,32},{32,64},{64,96},{96,0},{1,33},{33,65},{65,97},{97,1},{2,34}... | collective-permute-start | bytes 786440 | tf_op jit(solution)/shard_map/ppermute | solution.py:205
  77.2 19.0 %collective-permute-start.11 = (bf16[64,2048]{1,0:T(8,128)(2,1)S(1)}, bf16[64,2048]{1,0:T(8,128)(2,1)S(1)}, u32[]{:S(2)}, u32[]{:S(2)}) collective-permute-start(bf16[64,2048]{1,0:T(8,128)(2,1)S(1)} %get-tuple-element.34), channel_id=1, source_target_pairs={{0,96},{32,0},{64,32},{96,64},{1,97},{33,1},{65,33},{97,65},{2,98}... | collective-permute-start | bytes 786440 | tf_op jit(solution)/shard_map/ppermute | solution.py:205
  79.5 16.8 %collective-permute-start.10 = (bf16[64,2048]{1,0:T(8,128)(2,1)S(1)}, bf16[64,2048]{1,0:T(8,128)(2,1)S(1)}, u32[]{:S(2)}, u32[]{:S(2)}) collective-permute-start(bf16[64,2048]{1,0:T(8,128)(2,1)S(1)} %get-tuple-element.33), channel_id=1, source_target_pairs={{0,64},{32,96},{64,0},{96,32},{1,65},{33,97},{65,1},{97,33},{2,66}... | collective-permute-start | bytes 786440 | tf_op jit(solution)/shard_map/ppermute | solution.py:205
  82.5 18.3 %collective-permute-start.9 = (bf16[64,2048]{1,0:T(8,128)(2,1)S(1)}, bf16[64,2048]{1,0:T(8,128)(2,1)}, u32[]{:S(2)}, u32[]{:S(2)}) collective-permute-start(bf16[64,2048]{1,0:T(8,128)(2,1)S(1)} %get-tuple-element.32), channel_id=1, source_target_pairs={{0,32},{32,64},{64,96},{96,0},{1,33},{33,65},{65,97},{97,1},{2,34}... | collective-permute-start | bytes 786440 | tf_op jit(solution)/shard_map/ppermute | solution.py:205
  105.1 28.0 %all-to-all-start.4 = ((bf16[32,24,1024]{2,1,0:T(8,128)(2,1)}), bf16[32,24,1024]{2,1,0:T(8,128)(2,1)S(1)}, u32[]{:S(2)}, u32[]{:S(2)}) async-start(bf16[32,24,1024]{2,1,0:T(8,128)(2,1)} %bitcast.121), calls=%async_computation.4 | async-start | bytes 3145728 | tf_op jit(solution)/shard_map/all_to_all | solution.py:223
  112.0 22.2 %collective-permute-start.12 = (bf16[64,4096]{1,0:T(8,128)(2,1)}, bf16[64,4096]{1,0:T(8,128)(2,1)}, u32[]{:S(2)}, u32[]{:S(2)}) collective-permute-start(bf16[64,4096]{1,0:T(8,128)(2,1)} %multiply_convert_fusion), channel_id=1, source_target_pairs={{0,96},{32,0},{64,32},{96,64},{1,97},{33,1},{65,33},{97,65},{2,98}... | collective-permute-start | bytes 1572872 | tf_op jit(solution)/shard_map/ppermute | solution.py:205
  112.3 21.9 %collective-permute-start.13 = (bf16[64,4096]{1,0:T(8,128)(2,1)}, bf16[64,4096]{1,0:T(8,128)(2,1)}, u32[]{:S(2)}, u32[]{:S(2)}) collective-permute-start(bf16[64,4096]{1,0:T(8,128)(2,1)} %multiply_convert_fusion), channel_id=1, source_target_pairs={{0,64},{32,96},{64,0},{96,32},{1,65},{33,97},{65,1},{97,33},{2,66}... | collective-permute-start | bytes 1572872 | tf_op jit(solution)/shard_map/ppermute | solution.py:205
  112.8 26.4 %collective-permute-start.14 = (bf16[64,4096]{1,0:T(8,128)(2,1)}, bf16[64,4096]{1,0:T(8,128)(2,1)}, u32[]{:S(2)}, u32[]{:S(2)}) collective-permute-start(bf16[64,4096]{1,0:T(8,128)(2,1)} %multiply_convert_fusion), channel_id=1, source_target_pairs={{0,32},{32,64},{64,96},{96,0},{1,33},{33,65},{65,97},{97,1},{2,34}... | collective-permute-start | bytes 1572872 | tf_op jit(solution)/shard_map/ppermute | solution.py:205
  139.2 36.8 %collective-permute-start.15 = (bf16[192,4096]{1,0:T(8,128)(2,1)S(1)}, bf16[192,4096]{1,0:T(8,128)(2,1)}, u32[]{:S(2)}, u32[]{:S(2)}) collective-permute-start(bf16[192,4096]{1,0:T(8,128)(2,1)S(1)} %reshape.304.refs_0_), channel_id=1, source_target_pairs={{0,32},{32,64},{64,96},{96,0},{1,33},{33,65},{65,97},{97,1},{2,34}... | collective-permute-start | bytes 4718600 | tf_op jit(solution)/shard_map/ppermute | solution.py:205
  139.2 38.1 %collective-permute-start.17 = (bf16[192,4096]{1,0:T(8,128)(2,1)S(1)}, bf16[192,4096]{1,0:T(8,128)(2,1)S(1)}, u32[]{:S(2)}, u32[]{:S(2)}) collective-permute-start(bf16[192,4096]{1,0:T(8,128)(2,1)S(1)} %reshape.304.refs_0_), channel_id=1, source_target_pairs={{0,96},{32,0},{64,32},{96,64},{1,97},{33,1},{65,33},{97,65},{2,98}... | collective-permute-start | bytes 4718600 | tf_op jit(solution)/shard_map/ppermute | solution.py:205
  148.0 58.4 %all-to-all-start.5 = ((bf16[32,16,4096]{2,1,0:T(8,128)(2,1)}), bf16[32,16,4096]{2,1,0:T(8,128)(2,1)}, u32[]{:S(2)}, u32[]{:S(2)}) async-start(bf16[32,16,4096]{2,1,0:T(8,128)(2,1)} %bitcast.122), calls=%async_computation.5 | async-start | bytes 8388608 | tf_op jit(solution)/shard_map/all_to_all | solution.py:223
  156.1 116.6 %reduce-scatter.2.cloned.1.call-start = ((), (), s32[]{:S(2)}) async-start(), calls=%async_computation.10 | async-start | bytes 7864320 | tf_op jit(solution)/shard_map/reduce_scatter | solution.py:367
  177.2 19.7 %collective-permute-start.16 = (bf16[96,4096]{1,0:T(8,128)(2,1)S(1)}, bf16[96,4096]{1,0:T(8,128)(2,1)S(1)}, u32[]{:S(2)}, u32[]{:S(2)}) collective-permute-start(bf16[96,4096]{1,0:T(8,128)(2,1)S(1)} %slice.94), channel_id=1, source_target_pairs={{0,32},{32,64},{64,96},{96,0},{1,33},{33,65},{65,97},{97,1},{2,34}... | collective-permute-start | bytes 2359304 | tf_op jit(solution)/shard_map/ppermute | solution.py:205
  177.3 19.5 %collective-permute-start.18 = (bf16[96,4096]{1,0:T(8,128)(2,1)S(1)}, bf16[96,4096]{1,0:T(8,128)(2,1)S(1)}, u32[]{:S(2)}, u32[]{:S(2)}) collective-permute-start(bf16[96,4096]{1,0:T(8,128)(2,1)S(1)} %slice.95), channel_id=1, source_target_pairs={{0,96},{32,0},{64,32},{96,64},{1,97},{33,1},{65,33},{97,65},{2,98}... | collective-permute-start | bytes 2359304 | tf_op jit(solution)/shard_map/ppermute | solution.py:205
  222.6 58.7 %all-to-all-start.7 = ((bf16[32,16,4096]{2,1,0:T(8,128)(2,1)}), bf16[32,16,4096]{2,1,0:T(8,128)(2,1)}, u32[]{:S(2)}, u32[]{:S(2)}) async-start(bf16[32,16,4096]{2,1,0:T(8,128)(2,1)} %bitcast.123), calls=%async_computation.8 | async-start | bytes 8388608 | tf_op jit(solution)/shard_map/all_to_all | solution.py:223
  281.3 29.4 %all-to-all-start.6 = ((bf16[32,24,1024]{2,1,0:T(8,128)(2,1)}), bf16[32,24,1024]{2,1,0:T(8,128)(2,1)S(1)}, u32[]{:S(2)}, u32[]{:S(2)}) async-start(bf16[32,24,1024]{2,1,0:T(8,128)(2,1)} %reshape.307), calls=%async_computation.7 | async-start | bytes 3145728 | tf_op jit(solution)/shard_map/all_to_all | solution.py:223
  300.3 25.0 %collective-permute-start.21 = (bf16[64,4096]{1,0:T(8,128)(2,1)}, bf16[64,4096]{1,0:T(8,128)(2,1)S(1)}, u32[]{:S(2)}, u32[]{:S(2)}) collective-permute-start(bf16[64,4096]{1,0:T(8,128)(2,1)} %convolution_convert_fusion.1), channel_id=1, source_target_pairs={{0,96},{32,0},{64,32},{96,64},{1,97},{33,1},{65,33},{97,65},{2,98}... | collective-permute-start | bytes 1572872 | tf_op jit(solution)/shard_map/ppermute | solution.py:205
  302.9 22.4 %collective-permute-start.20 = (bf16[64,4096]{1,0:T(8,128)(2,1)}, bf16[64,4096]{1,0:T(8,128)(2,1)}, u32[]{:S(2)}, u32[]{:S(2)}) collective-permute-start(bf16[64,4096]{1,0:T(8,128)(2,1)} %convolution_convert_fusion.2), channel_id=1, source_target_pairs={{0,64},{32,96},{64,0},{96,32},{1,65},{33,97},{65,1},{97,33},{2,66}... | collective-permute-start | bytes 1572872 | tf_op jit(solution)/shard_map/ppermute | solution.py:205
  302.9 26.3 %collective-permute-start.19 = (bf16[64,4096]{1,0:T(8,128)(2,1)}, bf16[64,4096]{1,0:T(8,128)(2,1)}, u32[]{:S(2)}, u32[]{:S(2)}) collective-permute-start(bf16[64,4096]{1,0:T(8,128)(2,1)} %convolution_convert_fusion.3), channel_id=1, source_target_pairs={{0,32},{32,64},{64,96},{96,0},{1,33},{33,65},{65,97},{97,1},{2,34}... | collective-permute-start | bytes 1572872 | tf_op jit(solution)/shard_map/ppermute | solution.py:205
  (17 other events, 320.6 us)
Sparse Core Ops, SparseCore 0:
  9.6 56.6 all-gather.1
  206.5 66.1 reduce-scatter.1
